TPU v7x, 128 devices: a whole 4x4x4 slice. The times are simulated.
128 devices in a mesh: bra: 16 (over z, y), ket: 8 (over x, core).
Axes of the slice: x: 4, y: 4, z: 4, core: 2. Of those that a mesh axis runs over, the one named last changes fastest.
Arguments:
- quartet_tasks: int32 [16, 8, 512, 4], P('bra', 'ket'), may hold values from 0 to 767, as said below
- factors: bfloat16 [768, 16, 128], replicated, may hold values from -4.5 to 4.5
- density: bfloat16 [768, 96, 8, 256], P('bra', None, 'ket'), may hold values from -6 to 6
Outputs:
- fock_matrix: float32 [768, 96, 8, 256], P('bra', None, 'ket')
Inputs may be any that keep to these rules, and one draw needn't show every extreme that they name: `quartet_tasks`: entries are shell numbers. On the device with bra index b and ket index k, every task's i lies among b * 48 to (b + 1) * 48 - 1 and its d has d % 8 == k. Within each half of a device's task list (the first 256 tasks and the rest), the shells c and j of all its tasks name row blocks of one bra index at most 96 times and share one remainder mod 8 at most 80 times; both bounds are reached in each half of every device's list, by the same bra index and the same remainder in both halves.
All inputs are finite; a program needn't handle non-finite values.
Results may differ from a plain program's by a relative error of at most 0.0066.
Values may be sent and summed in bfloat16 or wider, within the bound.
No kernel may reach another device: no remote copies, remote signals or barrier semaphores. Data moves between devices by JAX's collectives and lax.ppermute only.
A program may use at most 64 MiB of HBM per device.

v0:
```python
import jax
import jax.numpy as jnp
from jax import lax
from jax.sharding import PartitionSpec as P

tile_scale = 0.0625


def pair_vectors(left_shell, right_shell):
    shell_count, basis_functions, terms = left_shell.shape
    joined = left_shell[:, :, None, :].astype(jnp.float32) * right_shell[:, None, :, :].astype(
        jnp.float32
    )
    return joined.reshape(shell_count, basis_functions * basis_functions, terms).astype(
        jnp.bfloat16
    )


def quartet_terms(factors, task_group, dens_cd, density_block_jd):
    group_member_count = task_group.shape[0]
    basis_functions = factors.shape[1]
    block_size = basis_functions * basis_functions
    bra_vec = pair_vectors(factors[task_group[:, 0]], factors[task_group[:, 1]])
    ket_vec = pair_vectors(factors[task_group[:, 2]], factors[task_group[:, 3]])
    raw_products = jnp.einsum("tpr,tqr->tpq", bra_vec, ket_vec, preferred_element_type=jnp.float32)
    integral_tile = (
        tile_scale * raw_products * lax.rsqrt(1.0 + raw_products * raw_products)
    ).astype(jnp.bfloat16)
    coulomb = jnp.einsum("tpq,tq->tp", integral_tile, dens_cd, preferred_element_type=jnp.float32)
    tile_rows = integral_tile.reshape(
        group_member_count, basis_functions, basis_functions, block_size
    ).astype(jnp.float32)
    density_rows = density_block_jd.reshape(
        group_member_count, basis_functions, basis_functions
    ).astype(jnp.float32)
    spread_rows = jnp.broadcast_to(
        density_rows[:, :, None, :],
        (group_member_count, basis_functions, basis_functions, basis_functions),
    ).reshape(group_member_count, basis_functions, block_size)
    summed_rows = jnp.sum(tile_rows * spread_rows[:, None, :, :], axis=2)
    exchange_contribution = jnp.sum(
        summed_rows.reshape(group_member_count, basis_functions, basis_functions, basis_functions),
        axis=3,
    )
    return (coulomb, exchange_contribution.reshape(group_member_count, block_size))


def evaluate(factors, quartets, dens_cd, density_block_jd):
    task_count = quartets.shape[0]
    block_size = dens_cd.shape[1]
    group_width = min(32, task_count)

    def one_group(packed):
        return quartet_terms(factors, packed[0], packed[1], packed[2])

    coulomb, exchange_contribution = lax.map(
        one_group,
        (
            quartets.reshape(-1, group_width, 4),
            dens_cd.reshape(-1, group_width, block_size),
            density_block_jd.reshape(-1, group_width, block_size),
        ),
    )
    return (
        coulomb.reshape(task_count, block_size),
        exchange_contribution.reshape(task_count, block_size),
    )


def bucket_slots(owners, count_of_owners, capacity):
    owner_marks = (owners[:, None] == jnp.arange(count_of_owners, dtype=jnp.int32)[None, :]).astype(
        jnp.int32
    )
    places = jnp.sum((jnp.cumsum(owner_marks, axis=0) - 1) * owner_marks, axis=1)
    return owners * capacity + places


def request_layout(density, shells, columns, capacity):
    bra_count = lax.axis_size("bra")
    rows_per_device, cols_dev = (density.shape[0], density.shape[1])
    owners = shells // rows_per_device
    slot_index = bucket_slots(owners, bra_count, capacity)
    wanted = shells % rows_per_device * cols_dev + columns
    asked_ids = (
        jnp.zeros((bra_count * capacity,), jnp.int32)
        .at[slot_index]
        .set(wanted)
        .reshape(bra_count, capacity)
    )
    block_table = density.reshape(rows_per_device * cols_dev, density.shape[3])
    return (slot_index, asked_ids, block_table)


def fetch_portion(density, shells, columns, capacity):
    slot_index, asked_ids, block_table = request_layout(density, shells, columns, capacity)
    answered = lax.all_to_all(
        block_table[lax.all_to_all(asked_ids, "bra", split_axis=0, concat_axis=0, tiled=True)],
        "bra",
        split_axis=0,
        concat_axis=0,
        tiled=True,
    )
    return answered.reshape(-1, density.shape[3])[slot_index]


def body(quartet_tasks, factors, density):
    quartets = quartet_tasks.reshape(-1, 4)
    task_count = quartets.shape[0]
    bra_count = lax.axis_size("bra")
    ket_count = lax.axis_size("ket")
    rows_per_device, cols_dev, block_size = (density.shape[0], density.shape[1], density.shape[3])
    wanted_rows = jnp.stack([quartets[:, 2], quartets[:, 1]], axis=1).reshape(-1)
    wanted_cols = jnp.repeat(quartets[:, 3] // ket_count, 2)
    halfway = task_count // 2
    coulomb_parts = []
    exchange_parts = []
    for portion in range(2):
        lower = portion * halfway
        upper = lower + halfway
        fetched = fetch_portion(
            density,
            wanted_rows[2 * lower : 2 * upper],
            wanted_cols[2 * lower : 2 * upper],
            3 * task_count // bra_count,
        ).reshape(halfway, 2, block_size)
        portion_coulomb, portion_exchange = evaluate(
            factors, quartets[lower:upper], fetched[:, 0], fetched[:, 1]
        )
        coulomb_parts.append(portion_coulomb)
        exchange_parts.append(portion_exchange)
    coulomb = jnp.concatenate(coulomb_parts, axis=0)
    exchange_contribution = jnp.concatenate(exchange_parts, axis=0)
    targets = jnp.stack([quartets[:, 1], quartets[:, 2]], axis=1).reshape(-1)
    contributions = jnp.stack([coulomb, -0.5 * exchange_contribution], axis=1).reshape(
        -1, block_size
    )
    bra_rows = jnp.repeat(quartets[:, 0] % rows_per_device, 2)
    owners = targets % ket_count
    capacity = 5 * task_count // (2 * ket_count)
    slot_index = bucket_slots(owners, ket_count, capacity)
    positions = bra_rows * cols_dev + targets // ket_count
    outgoing = (
        jnp.zeros((ket_count * capacity, block_size), jnp.float32)
        .at[slot_index]
        .set(contributions)
        .reshape(ket_count, capacity, block_size)
    )
    out_index = (
        jnp.zeros((ket_count * capacity,), jnp.int32)
        .at[slot_index]
        .set(positions)
        .reshape(ket_count, capacity)
    )
    received_blocks, arrived_index = (
        lax.all_to_all(outgoing, "ket", split_axis=0, concat_axis=0, tiled=True),
        lax.all_to_all(out_index, "ket", split_axis=0, concat_axis=0, tiled=True),
    )
    fock_matrix = (
        jnp.zeros((rows_per_device * cols_dev, block_size), jnp.float32)
        .at[arrived_index.reshape(-1)]
        .add(received_blocks.reshape(-1, block_size))
    )
    return fock_matrix.reshape(rows_per_device, cols_dev, 1, block_size)


def solution(mesh):
    placed = (P("bra", "ket", None, None), P(), P("bra", None, "ket", None))
    return jax.shard_map(
        body, mesh=mesh, in_specs=placed, out_specs=P("bra", None, "ket", None), check_vma=False
    )
```

profile of v0, /device:TPU:1, one launch (start us, length us, event | category | flops | bytes accessed | tf_op | source)
XLA Modules:
  0.0 619.3 jit_solution(18121270472420547491)
XLA Ops:
  7.7 8.6 %all-to-all-start.1 = ((s32[16,1,96]{2,1,0:T(1,128)}), s32[16,1,96]{2,1,0:T(1,128)S(1)}, u32[]{:S(2)}, u32[]{:S(2)}) async-start(s32[16,1,96]{2,1,0:T(1,128)} %all_to_all.33), calls=%async_computation.1 | async-start | bytes 16384 | tf_op jit(solution)/shard_map/all_to_all | solution.py:97
  28.9 6.7 %all-to-all-start.3 = ((s32[16,1,96]{2,1,0:T(1,128)}), s32[16,1,96]{2,1,0:T(1,128)S(1)}, u32[]{:S(2)}, u32[]{:S(2)}) async-start(s32[16,1,96]{2,1,0:T(1,128)} %all_to_all.37), calls=%async_computation.3 | async-start | bytes 16384 | tf_op jit(solution)/shard_map/all_to_all | solution.py:97
  42.0 5.7 all-to-all-start.2
  60.2 5.4 all-to-all-start.4
  70.1 244.7 %while.24 = (s32[]{:T(128)}, f32[8,32,256]{2,1,0:T(8,128)}, f32[8,32,256]{2,1,0:T(8,128)}, s32[8,32,4]{1,0,2:T(8,128)}, bf16[768,16,128]{2,1,0:T(8,128)(2,1)}, /...) while((s32[]{:T(128)}, f32[8,32,256]{2,1,0:T(8,128)}, ...), condition=%wide.region_11.12_spmd, body=%wide.region_8.11_spmd.sunk | while | flops 562295168 | bytes 25054816 | solution.py:56
  89.4 5.4 fusion.84
  120.0 5.4 fusion.84
  150.6 5.4 fusion.84
  181.1 5.4 fusion.84
  211.7 5.4 fusion.84
  242.3 5.4 fusion.84
  272.9 5.4 fusion.84
  303.5 5.4 fusion.84
  314.8 6.9 %all-to-all-start = ((s32[8,1,160]{2,1,0:T(1,128)}), s32[8,1,160]{2,1,0:T(1,128)}, u32[]{:S(2)}, u32[]{:S(2)}) async-start(s32[8,1,160]{2,1,0:T(1,128)} %all_to_all.31), calls=%async_computation | async-start | bytes 16384 | tf_op jit(solution)/shard_map/all_to_all | solution.py:156
  327.2 238.9 %while.25 = (s32[]{:T(128)}, f32[8,32,256]{2,1,0:T(8,128)}, f32[8,32,256]{2,1,0:T(8,128)}, s32[8,32,4]{1,0,2:T(8,128)S(1)}, bf16[768,16,128]{2,1,0:T(8,128)(2,1)...) while((s32[]{:T(128)}, f32[8,32,256]{2,1,0:T(8,128)}, ...), condition=%wide.region_19.20_spmd, body=%wide.region_16.19_spmd.sunk | while | flops 562295168 | bytes 25054816 | solution.py:56
  345.8 5.4 fusion.91
  375.6 5.4 fusion.91
  465.2 5.4 fusion.91
  495.1 5.4 fusion.91
  554.8 5.4 fusion.91
  570.9 6.4 %scatter_custom_fusion.3 = f32[1280,256]{1,0:T(8,128)} fusion(s32[1024]{0:T(1024)} %bitcast.238, f32[1024,256]{1,0:T(8,128)} %reshape.770, f32[]{:T(128)} %constant.127.clone.1), kind=kCustom, calls=%fused_computation.70 | custom fusion | bytes 1311232 | tf_op jit(solution)/shard_map/scatter | solution.py:145
  583.1 17.0 %all-to-all-done.5 = f32[8,160,256]{2,1,0:T(8,128)} async-done(((f32[8,160,256]{2,1,0:T(8,128)}), f32[8,160,256]{2,1,0:T(8,128)}, u32[]{:S(2)}, u32[]{:S(2)}) %all-to-all-start.5) | async-done | bytes 1310752 | tf_op jit(solution)/shard_map/all_to_all | solution.py:155
  600.2 11.3 %scatter_custom_fusion.4 = f32[4608,256]{1,0:T(8,128)} fusion(s32[1280]{0:T(1024)S(1)} %fusion.27, f32[1280,256]{1,0:T(8,128)} %bitcast.61, f32[]{:T(128)} %constant.127.clone.1), kind=kCustom, calls=%fused_computation.67 | custom fusion | flops 327680 | bytes 4719104 | tf_op jit(solution)/shard_map/scatter-add | solution.py:161
  611.5 7.8 %reshape.641 = f32[48,96,1,256]{3,2,1,0:T(1,128)} reshape(f32[4608,256]{1,0:T(8,128)} %scatter_custom_fusion.4) | data formatting | bytes 9437184 | tf_op jit(solution)/shard_map/reshape | solution.py:163
  (537 shorter events, 471.8 us)
Async XLA Ops:
  0.0 35.7 %copy-start = (bf16[48,96,1,256]{3,1,2,0:T(8,128)(2,1)S(1)}, bf16[48,96,1,256]{3,1,2,0:T(8,128)(2,1)}, u32[]{:S(2)}) copy-start(bf16[48,96,1,256]{3,1,2,0:T(8,128)(2,1)} %param.9) | copy-start | bytes 7077892
  7.7 21.3 %all-to-all-start.1 = ((s32[16,1,96]{2,1,0:T(1,128)}), s32[16,1,96]{2,1,0:T(1,128)S(1)}, u32[]{:S(2)}, u32[]{:S(2)}) async-start(s32[16,1,96]{2,1,0:T(1,128)} %all_to_all.33), calls=%async_computation.1 | async-start | bytes 16384 | tf_op jit(solution)/shard_map/all_to_all | solution.py:97
  28.9 13.1 %all-to-all-start.3 = ((s32[16,1,96]{2,1,0:T(1,128)}), s32[16,1,96]{2,1,0:T(1,128)S(1)}, u32[]{:S(2)}, u32[]{:S(2)}) async-start(s32[16,1,96]{2,1,0:T(1,128)} %all_to_all.37), calls=%async_computation.3 | async-start | bytes 16384 | tf_op jit(solution)/shard_map/all_to_all | solution.py:97
  42.0 18.1 %all-to-all-start.2 = ((bf16[16,96,256]{2,1,0:T(8,128)(2,1)}), bf16[16,96,256]{2,1,0:T(8,128)(2,1)S(1)}, u32[]{:S(2)}, u32[]{:S(2)}) async-start(bf16[16,96,256]{2,1,0:T(8,128)(2,1)} %bitcast.214), calls=%async_computation.2 | async-start | bytes 1572864 | tf_op jit(solution)/shard_map/all_to_all | solution.py:96
  47.8 12.4 %copy-start.1 = (s32[1024,1]{0,1:T(1,128)}, s32[1024,1]{0,1:T(1,128)S(1)}, u32[]{:S(2)}) copy-start(s32[1024,1]{0,1:T(1,128)S(1)} %compare_select_fusion.9) | copy-start | bytes 12292
  60.2 254.6 %all-to-all-start.4 = ((bf16[16,96,256]{2,1,0:T(8,128)(2,1)}), bf16[16,96,256]{2,1,0:T(8,128)(2,1)}, u32[]{:S(2)}, u32[]{:S(2)}) async-start(bf16[16,96,256]{2,1,0:T(8,128)(2,1)} %bitcast.213), calls=%async_computation.4 | async-start | bytes 1572864 | tf_op jit(solution)/shard_map/all_to_all | solution.py:96
  314.8 262.5 %all-to-all-start = ((s32[8,1,160]{2,1,0:T(1,128)}), s32[8,1,160]{2,1,0:T(1,128)}, u32[]{:S(2)}, u32[]{:S(2)}) async-start(s32[8,1,160]{2,1,0:T(1,128)} %all_to_all.31), calls=%async_computation | async-start | bytes 16384 | tf_op jit(solution)/shard_map/all_to_all | solution.py:156
  577.3 22.9 %all-to-all-start.5 = ((f32[8,160,256]{2,1,0:T(8,128)}), f32[8,160,256]{2,1,0:T(8,128)}, u32[]{:S(2)}, u32[]{:S(2)}) async-start(f32[8,160,256]{2,1,0:T(8,128)} %bitcast.212), calls=%async_computation.5 | async-start | bytes 2621440 | tf_op jit(solution)/shard_map/all_to_all | solution.py:155
where the time goes:
time: 625 us; the launch traced here: 619 us
  local copies, waits for them, and re-layouts  338 us (54%)
  other arithmetic  117 us (19%)
  matrix products  105 us (17%)
  starting transfers between devices  38.2 us (6%)
  waiting for transfers between devices  19.3 us (3%)
    dot_general x16, matrix products, quartet_terms(): jnp.einsum('tpr,tqr->tpq', bra_vec, ket_vec, preferred_element_type=jnp.f...  85.9 us
    gather x32, local copies, waits for them, and re-layouts, quartet_terms(): bra_vec = pair_vectors(factors[task_group[:, 0]], factors[task_group[:, 1]])  79.4 us
    gather x32, local copies, waits for them, and re-layouts, quartet_terms(): ket_vec = pair_vectors(factors[task_group[:, 2]], factors[task_group[:, 3]])  79.4 us
    convert_element_type x32, other arithmetic, pair_vectors(): joined.reshape(shell_count, basis_functions * basis_functions, terms)  60.9 us
    mul x16, local copies, waits for them, and re-layouts, quartet_terms(): summed_rows = jnp.sum(tile_rows * spread_rows[:, None, :, :], axis=2)  36.4 us
    reduce_sum x16, other arithmetic, quartet_terms(): jnp.sum(summed_rows.reshape(group_member_count, basis_functions, basis_fu...  33.1 us
    reduce_sum x16, local copies, waits for them, and re-layouts, quartet_terms(): summed_rows = jnp.sum(tile_rows * spread_rows[:, None, :, :], axis=2)  31.8 us
    broadcast_in_dim x16, local copies, waits for them, and re-layouts, quartet_terms(): jnp.broadcast_to(density_rows[:, :, None, :], (group_member_count, basis_...  23.8 us
  transfers between devices with their start and end apart: 6, of which 3 were waited for; matrix products, arithmetic and copies ran while one was open for 86% of the time, Pallas kernels for 0%

commit v1 on v0

v1 whole, which is shorter than its diff:
```python
import functools

import jax
import jax.numpy as jnp
import numpy as np
from jax import lax
from jax.experimental import pallas as pl
from jax.experimental.pallas import tpu as pltpu
from jax.sharding import PartitionSpec as P

F32, BF16, I32 = jnp.float32, jnp.bfloat16, jnp.int32
FUNCS, RANK, BSZ = 16, 128, 256
NBLK, ROWB, COLB = 768, 48, 96
NBRA, NKET, TASKS = 16, 8, 512
HALF, CAPB, CAPK = 256, 96, 80
OUTROWS = 96
GROUP = 16
NB = ROWB * COLB
VM = pl.BlockSpec(memory_space=pltpu.VMEM)
SM = pl.BlockSpec(memory_space=pltpu.SMEM)
PARAMS = pltpu.CompilerParams(vmem_limit_bytes=60 * 1024 * 1024)


def iota(shape, dim):
    return lax.broadcasted_iota(I32, shape, dim)


def nt_dot(a, b):
    return lax.dot_general(a, b, (((1,), (1,)), ((), ())), preferred_element_type=F32)


def ranks(owners, count, upper, carry):
    marks = (iota((count, HALF), 0) == owners).astype(F32)
    before = jnp.dot(marks.astype(BF16), upper, preferred_element_type=F32) + carry
    place = jnp.sum(before * marks, axis=0, keepdims=True).astype(I32)
    return marks, place, carry + jnp.sum(marks, axis=1, keepdims=True)


def table(marks, place, value, width):
    at = (iota((width, HALF), 0) == place).astype(BF16)
    high = (value // 64).astype(F32)
    low = (value % 64).astype(F32)
    return nt_dot((marks * high).astype(BF16), at), nt_dot((marks * low).astype(BF16), at)


def prep_kernel(tasks, ids, slots, oslots, places):
    upper = (iota((HALF, HALF), 0) < iota((HALF, HALF), 1)).astype(BF16)
    for h in range(2):
        i, j, c, d = (tasks[r : r + 1, h * HALF : (h + 1) * HALF] for r in range(4))
        carry = jnp.zeros((NBRA, 1), F32)
        high = low = 0.0
        for k, s in enumerate((c, j)):
            own = s // ROWB
            marks, place, carry = ranks(own, NBRA, upper, carry)
            slots[k : k + 1, h * HALF : (h + 1) * HALF] = own * CAPB + place
            a, b = table(marks, place, (s % ROWB) * COLB + d // NKET, 128)
            high, low = high + a, low + b
        got = (high * 64.0 + low).astype(I32)
        ids[:, h * 128 : (h + 1) * 128] = jnp.where(iota((NBRA, 128), 1) < CAPB, got, carry.astype(I32))
        carry = jnp.zeros((NKET, 1), F32)
        high = low = 0.0
        for k, s in enumerate((j, c)):
            own = s % NKET
            marks, place, carry = ranks(own, NKET, upper, carry)
            oslots[k : k + 1, h * HALF : (h + 1) * HALF] = own * CAPK + place
            a, b = table(marks, place, (i % ROWB) * COLB + s // NKET + 1, 128)
            high, low = high + a, low + b
        places[h, :, 0:128] = high
        places[h, :, 128:256] = low


def prep(tasks):
    return pl.pallas_call(
        prep_kernel,
        out_shape=(
            jax.ShapeDtypeStruct((NBRA, 256), I32),
            jax.ShapeDtypeStruct((2, TASKS), I32),
            jax.ShapeDtypeStruct((2, TASKS), I32),
            jax.ShapeDtypeStruct((2, NKET, 256), F32),
        ),
        in_specs=[VM],
        out_specs=(VM,) * 4,
        compiler_params=PARAMS,
    )(tasks)


def spread(src, dst, rows):
    def step(k, _):
        for u in range(4):
            r = pl.multiple_of(k * 64 + u * 16, 16)
            v = src[pl.ds(r, 16), :].astype(F32)
            dst[pl.ds(2 * r, 16, stride=2), :] = v[:, :128]
            dst[pl.ds(2 * r + 1, 16, stride=2), :] = v[:, 128:]
        return 0

    lax.fori_loop(0, rows // 64, step, 0)


def gather_kernel(half, ids, dens, out, wide, got):
    spread(dens, wide, NB)

    def source(s, _):
        count = ids[s, half * 128 + CAPB]

        def step(k, _):
            for u in range(8):
                p = k * 8 + u
                r = ids[s, half * 128 + p]
                got[pl.ds((s * CAPB + p) * 2, 2), :] = wide[pl.ds(r * 2, 2), :]
            return 0

        lax.fori_loop(0, (count + 7) // 8, step, 0)
        return 0

    lax.fori_loop(0, NBRA, source, 0)

    def pack(k, _):
        for u in range(4):
            r = pl.multiple_of(k * 64 + u * 16, 16)
            out[pl.ds(r, 16), 0:128] = got[pl.ds(2 * r, 16, stride=2), :].astype(BF16)
            out[pl.ds(r, 16), 128:256] = got[pl.ds(2 * r + 1, 16, stride=2), :].astype(BF16)
        return 0

    lax.fori_loop(0, NBRA * CAPB // 64, pack, 0)


def gather(half, ids, dens):
    return pl.pallas_call(
        functools.partial(gather_kernel, half),
        out_shape=jax.ShapeDtypeStruct((NBRA * CAPB, 256), BF16),
        in_specs=[SM, VM],
        out_specs=VM,
        scratch_shapes=[pltpu.VMEM((2 * NB, 128), F32), pltpu.VMEM((2 * NBRA * CAPB, 128), F32)],
        compiler_params=PARAMS,
    )(ids, dens)


def constants():
    r = np.arange(256)
    lane = np.arange(128)
    spread_b = r[:, None] // 16 == lane[None, :] % 16
    sum_f = np.arange(16)[:, None] == r[None, :] // 16
    sum_b = r[:, None] // 16 == r[None, :] // 16
    keep_f = np.arange(16)[:, None] == lane[None, :] % 16
    return [jnp.asarray(x, BF16) for x in (spread_b, sum_f, sum_b)] + [jnp.asarray(keep_f, F32)]


def eval_kernel(
    half, tasks, slots, oslots, fac, fetched, places, spread_b, sum_f, sum_b, keep_f, out,
    rows, wide, outw, cd, jd, dsp, part, fin,
):
    base = half * HALF

    def widen(k, _):
        for u in range(8):
            rows[pl.ds(pl.multiple_of((k * 8 + u) * 16, 16), 16), :] = fac[k * 8 + u].astype(F32)
        return 0

    lax.fori_loop(0, NBLK // 8, widen, 0)
    spread(fetched, wide, NBRA * CAPB)
    keep = keep_f[...]

    def pairs(x, y):
        fy = fac[y]
        return jnp.concatenate(
            [
                jnp.broadcast_to(rows[pl.ds(x * FUNCS + a, 1), :], (FUNCS, RANK)).astype(BF16) * fy
                for a in range(FUNCS)
            ],
            axis=0,
        )

    def group(g, _):
        for n in range(GROUP):
            t = base + g * GROUP + n
            cd[2 * n : 2 * n + 2, :] = wide[pl.ds(slots[0, t] * 2, 2), :]
            block = wide[pl.ds(slots[1, t] * 2, 2), :]
            jd[n * 16 : n * 16 + 16, 0:128] = (jnp.broadcast_to(block[0:1], (16, 128)) * keep).astype(BF16)
            jd[n * 16 : n * 16 + 16, 128:256] = (jnp.broadcast_to(block[1:2], (16, 128)) * keep).astype(BF16)
        dsp[...] = jnp.dot(jd[...], spread_b[...], preferred_element_type=F32).astype(BF16)
        dcd = jnp.concatenate([cd[pl.ds(0, 16, stride=2), :], cd[pl.ds(1, 16, stride=2), :]], axis=1).astype(BF16)
        acc = jnp.zeros((GROUP, BSZ), F32)
        for n in range(GROUP):
            t = base + g * GROUP + n
            bra = pairs(tasks[0, t], tasks[1, t])
            ket = pairs(tasks[2, t], tasks[3, t])
            raw = nt_dot(ket, bra).astype(BF16)
            tile = raw * lax.rsqrt(raw * raw + BF16(1.0))
            coul = jnp.dot(dcd, tile, preferred_element_type=F32)
            acc = jnp.where(iota((GROUP, BSZ), 0) == n, coul, acc)
            dd = dsp[n * 16 : n * 16 + 16, :]
            dd = jnp.concatenate([dd, dd], axis=1)
            prod = jnp.concatenate([tile[16 * e : 16 * e + 16, :] * dd for e in range(16)], axis=0)
            part[n * 16 : n * 16 + 16, :] = jnp.dot(sum_f[...], prod, preferred_element_type=F32).astype(BF16)
        full = jnp.dot(part[...], sum_b[...], preferred_element_type=F32)
        full = jnp.where((iota((256, 256), 0) % 16) == (iota((256, 256), 1) % 16), full, 0.0)
        exch = jnp.dot(sum_f[...], full.astype(BF16), preferred_element_type=F32) * (-0.5 * 0.0625)
        acc = acc * 0.0625
        for k, v in enumerate((acc, exch)):
            fin[pl.ds(32 * k, 16, stride=2), :] = v[:, :128]
            fin[pl.ds(32 * k + 1, 16, stride=2), :] = v[:, 128:]
        for n in range(GROUP):
            t = base + g * GROUP + n
            for k in range(2):
                outw[pl.ds(oslots[k, t] * 2, 2), :] = fin[32 * k + 2 * n : 32 * k + 2 * n + 2, :]
        return 0

    lax.fori_loop(0, HALF // GROUP, group, 0)
    for o in range(NKET):
        for b in range(CAPK // 16):
            r = o * CAPK + b * 16
            for k in range(2):
                out[o, b * 16 : b * 16 + 16, 128 * k : 128 * k + 128] = outw[
                    pl.ds(2 * r + k, 16, stride=2), :
                ].astype(BF16)
        out[o, CAPK:OUTROWS, :] = jnp.broadcast_to(places[half, o : o + 1, :], (16, 256)).astype(BF16)


def evaluate(half, tasks, slots, oslots, factors, fetched, places):
    return pl.pallas_call(
        functools.partial(eval_kernel, half),
        out_shape=jax.ShapeDtypeStruct((NKET, OUTROWS, 256), BF16),
        in_specs=[SM] * 3 + [VM] * 7,
        out_specs=VM,
        scratch_shapes=[
            pltpu.VMEM((NBLK * FUNCS, RANK), F32),
            pltpu.VMEM((2 * NBRA * CAPB, 128), F32),
            pltpu.VMEM((2 * NKET * CAPK, 128), F32),
            pltpu.VMEM((2 * GROUP, 128), F32),
            pltpu.VMEM((256, 256), BF16),
            pltpu.VMEM((256, 128), BF16),
            pltpu.VMEM((256, 256), BF16),
            pltpu.VMEM((4 * GROUP, 128), F32),
        ],
        compiler_params=PARAMS,
    )(tasks, slots, oslots, factors, fetched, places, *constants())


SUMS = 4


def scatter_kernel(first, second, out, wide, where_v, where_s, sem, *accs):
    def clear(k, _):
        for u in range(4):
            r = pl.multiple_of((k * 4 + u) * 8, 8)
            for acc in accs:
                acc[pl.ds(r, 8), :] = jnp.zeros((8, 128), F32)
        return 0

    lax.fori_loop(0, 2 * NB // 32, clear, 0)
    for h, src in enumerate((first, second)):
        for o in range(NKET):
            at = h * NKET + o
            row = src[o, CAPK : CAPK + 16, :].astype(F32)
            pos = (row[0:1, 0:128] * 64.0 + row[0:1, 128:256]).astype(I32) - 1
            where_v[at : at + 1, :] = jnp.where(pos < 0, NB, pos)
            for b in range(CAPK // 16):
                r = at * CAPK + b * 16
                v = src[o, b * 16 : b * 16 + 16, :].astype(F32)
                wide[pl.ds(2 * r, 16, stride=2), :] = v[:, :128]
                wide[pl.ds(2 * r + 1, 16, stride=2), :] = v[:, 128:]
    copy = pltpu.make_async_copy(where_v, where_s, sem)
    copy.start()
    copy.wait()
    per = 2 * NKET // SUMS

    def source(s, _):
        def step(k, _):
            for u in range(8):
                p = k * 8 + u
                for q, acc in enumerate(accs):
                    at = q * per + s
                    r = where_s[at, p]
                    acc[pl.ds(2 * r, 2), :] += wide[pl.ds((at * CAPK + p) * 2, 2), :]
            return 0

        lax.fori_loop(0, CAPK // 8, step, 0)
        return 0

    lax.fori_loop(0, per, source, 0)

    def total(k, _):
        for u in range(4):
            r = pl.multiple_of((k * 4 + u) * 8, 8)
            v = accs[0][pl.ds(r, 8), :]
            for acc in accs[1:]:
                v = v + acc[pl.ds(r, 8), :]
            out[pl.ds(r, 8), :] = v
        return 0

    lax.fori_loop(0, 2 * NB // 32, total, 0)


def scatter(first, second):
    return pl.pallas_call(
        scatter_kernel,
        out_shape=jax.ShapeDtypeStruct((2 * NB, 128), F32),
        in_specs=[VM, VM],
        out_specs=VM,
        scratch_shapes=[
            pltpu.VMEM((4 * NKET * CAPK, 128), F32),
            pltpu.VMEM((2 * NKET, 128), I32),
            pltpu.SMEM((2 * NKET, 128), I32),
            pltpu.SemaphoreType.DMA,
        ]
        + [pltpu.VMEM((2 * NB + 8, 128), F32)] * SUMS,
        compiler_params=PARAMS,
    )(first, second)


def exchange(x, axis):
    return lax.all_to_all(x, axis, split_axis=0, concat_axis=0, tiled=True)


def body(quartet_tasks, factors, density):
    tasks = quartet_tasks.reshape(TASKS, 4).T
    dens = density.reshape(NB, BSZ)
    ids, slots, oslots, places = prep(tasks)
    asked = exchange(ids, "bra")
    fetched = []
    for h in range(2):
        blocks = gather(h, asked, dens)
        fetched.append(exchange(blocks.reshape(NBRA, CAPB, BSZ), "bra").reshape(NBRA * CAPB, BSZ))
    arrived = []
    for h in range(2):
        parts = evaluate(h, tasks, slots, oslots, factors, fetched[h], places)
        arrived.append(exchange(parts, "ket"))
    fock = scatter(arrived[0], arrived[1])
    return fock.reshape(ROWB, COLB, 1, BSZ)


def solution(mesh):
    placed = (P("bra", "ket", None, None), P(), P("bra", None, "ket", None))
    return jax.shard_map(
        body, mesh=mesh, in_specs=placed, out_specs=P("bra", None, "ket", None), check_vma=False
    )
```

time: 625 us -> 144 us (0.23)
  local copies, waits for them, and re-layouts: 338 us -> 1.34 us
  other arithmetic: 117 us -> 0 us
  matrix products: 105 us -> 0 us
  Pallas kernels: 0 us -> 93.1 us
  blocking collectives: 0 us -> 27.8 us
  starting transfers between devices: 38.2 us -> 14.3 us
  waiting for transfers between devices: 19.3 us -> 6.79 us
    gather x68 -> x0, local copies, waits for them, and re-layouts: 174 us -> none  [the longest x32 79.4 us: quartet_terms(): bra_vec = pair_vectors(factors[task_group[:, 0]], factors[task_group[:, 1]])]
    dot_general x32 -> x0, matrix products: 105 us -> none  [the longest x16 85.9 us: quartet_terms(): jnp.einsum('tpr,tqr->tpq', bra_vec, ket_vec, preferred_element_type=jnp.f...]
    pallas_call x0 -> x6, Pallas kernels: none -> 93.1 us  [the longest x2 68.6 us: evaluate(): pl.pallas_call(functools.partial(eval_kernel, half), out_shape=jax.ShapeD...]
    convert_element_type x99 -> x0, other arithmetic: 62.2 us -> none  [the longest x32 60.9 us: pair_vectors(): joined.reshape(shell_count, basis_functions * basis_functions, terms)]
    mul x17 -> x0, local copies, waits for them, and re-layouts: 36.6 us -> none  [the longest x16 36.4 us: quartet_terms(): summed_rows = jnp.sum(tile_rows * spread_rows[:, None, :, :], axis=2)]
    reduce_sum x19 -> x0, other arithmetic: 33.3 us -> none  [the longest x16 33.1 us: quartet_terms(): jnp.sum(summed_rows.reshape(group_member_count, basis_functions, basis_fu...]
    reduce_sum x16 -> x0, local copies, waits for them, and re-layouts: 31.8 us -> none  [quartet_terms(): summed_rows = jnp.sum(tile_rows * spread_rows[:, None, :, :], axis=2)]
    all_to_all x0 -> x2, blocking collectives: none -> 27.8 us  [exchange(): return lax.all_to_all(x, axis, split_axis=0, concat_axis=0, tiled=True)]
  transfers between devices with their start and end apart: 6 -> 3, of which waited for: 3 -> 1; matrix products, arithmetic and copies ran while one was open for 86% -> 0% of each run, Pallas kernels for 0% -> 52%
where the time goes in v1:
time: 144 us; the launch traced here: 143 us
  Pallas kernels  93.1 us (65%)
  blocking collectives  27.8 us (19%)
  starting transfers between devices  14.3 us (10%)
  waiting for transfers between devices  6.79 us (5%)
    pallas_call x2, Pallas kernels, evaluate(): pl.pallas_call(functools.partial(eval_kernel, half), out_shape=jax.ShapeD...  68.6 us
    all_to_all x2, blocking collectives, exchange(): return lax.all_to_all(x, axis, split_axis=0, concat_axis=0, tiled=True)  27.8 us
    all_to_all x3, starting transfers between devices, exchange(): return lax.all_to_all(x, axis, split_axis=0, concat_axis=0, tiled=True)  14.3 us
    pallas_call x2, Pallas kernels, gather(): pl.pallas_call(functools.partial(gather_kernel, half), out_shape=jax.Shap...  11.4 us
    pallas_call x1, Pallas kernels, scatter(): pl.pallas_call(scatter_kernel, out_shape=jax.ShapeDtypeStruct((2 * NB, 12...  10.8 us
    all_to_all x3, waiting for transfers between devices, exchange(): return lax.all_to_all(x, axis, split_axis=0, concat_axis=0, tiled=True)  6.79 us
  transfers between devices with their start and end apart: 3, of which 1 were waited for; matrix products, arithmetic and copies ran while one was open for 0% of the time, Pallas kernels for 52%

profile of v1, /device:TPU:1, one launch (start us, length us, event | category | flops | bytes accessed | tf_op | source)
XLA Modules:
  0.0 143.4 jit_solution(10794112752593505552)
XLA Ops:
  0.0 2.3 %shard_map.109 = (s32[16,256]{1,0:T(8,128)}, s32[2,512]{1,0:T(2,128)}, s32[2,512]{1,0:T(2,128)}, f32[2,8,256]{2,1,0:T(8,128)}) custom-call(s32[4,512]{1,0:T(4,128)} %bitcast.21), custom_call_target="tpu_custom_call" | custom-call | tf_op jit(solution)/shard_map/pallas_call | solution.py:73
  2.3 0.7 copy.13
  3.1 14.8 %all_to_all.31 = s32[16,1,256]{2,1,0:T(1,128)S(1)} all-to-all(s32[16,1,256]{2,1,0:T(1,128)S(1)} %copy.13), channel_id=1, replica_groups=mesh['bra'=16,'ket'=8] {'bra'}, dimensions={0} | all-to-all | bytes 32768 | tf_op jit(solution)/shard_map/all_to_all | solution.py:312
  17.9 0.6 copy.17
  18.5 5.7 %shard_map.112 = bf16[1536,256]{1,0:T(8,128)(2,1)} custom-call(s32[16,256]{1,0:T(8,128)} %bitcast.19, bf16[4608,256]{1,0:T(8,128)(2,1)} %bitcast.13), custom_call_target="tpu_custom_call" | custom-call | tf_op jit(solution)/shard_map/pallas_call | solution.py:128
  24.2 3.6 %all-to-all-start.3 = ((bf16[16,96,256]{2,1,0:T(8,128)(2,1)}), bf16[16,96,256]{2,1,0:T(8,128)(2,1)S(1)}, u32[]{:S(2)}, u32[]{:S(2)}) async-start(bf16[16,96,256]{2,1,0:T(8,128)(2,1)} %bitcast.18), calls=%async_computation.3 | async-start | bytes 1572864 | tf_op jit(solution)/shard_map/all_to_all | solution.py:312
  27.8 5.7 %shard_map.110 = bf16[1536,256]{1,0:T(8,128)(2,1)} custom-call(s32[16,256]{1,0:T(8,128)} %bitcast.20, bf16[4608,256]{1,0:T(8,128)(2,1)} %bitcast.14), custom_call_target="tpu_custom_call" | custom-call | tf_op jit(solution)/shard_map/pallas_call | solution.py:128
  33.5 6.8 %all-to-all-done.3 = bf16[16,96,256]{2,1,0:T(8,128)(2,1)S(1)} async-done(((bf16[16,96,256]{2,1,0:T(8,128)(2,1)}), bf16[16,96,256]{2,1,0:T(8,128)(2,1)S(1)}, u32[]{:S(2)}, u32[]{:S(2)}) %all-to-all-start.3) | async-done | bytes 786464 | tf_op jit(solution)/shard_map/all_to_all | solution.py:312
  40.3 0.0 copy-start.1
  40.3 3.6 %all-to-all-start.1 = ((bf16[16,96,256]{2,1,0:T(8,128)(2,1)}), bf16[16,96,256]{2,1,0:T(8,128)(2,1)S(1)}, u32[]{:S(2)}, u32[]{:S(2)}) async-start(bf16[16,96,256]{2,1,0:T(8,128)(2,1)} %bitcast.17), calls=%async_computation.1 | async-start | bytes 1572864 | tf_op jit(solution)/shard_map/all_to_all | solution.py:312
  43.9 0.0 copy-done.1
  44.0 34.3 %shard_map.113 = bf16[8,96,256]{2,1,0:T(8,128)(2,1)} custom-call(s32[4,512]{1,0:T(4,128)} %bitcast.22, s32[2,512]{1,0:T(2,128)} %get-tuple-element.9.slots, s32[2,512]{1,0:T(2,128)} %get-tuple-element.10.oslots, bf16[768,16,128]{2,1,0:T(8,128)(2,1)} %fac.3, bf16[1536,256]{1,0:T(8,128)(2,1)} %bitcast.16, f32[2,8,256]{2,1,0:T(8,128)} %get-tuple-element.12.places, ...), custom_call_target="tpu_custom_call" | custom-call | tf_op jit(solution)/shard_map/pallas_call | solution.py:220
  78.2 0.0 all-to-all-done.1
  78.2 0.0 copy-start
  78.2 7.1 %all-to-all-start.4 = ((bf16[8,96,256]{2,1,0:T(8,128)(2,1)}), bf16[8,96,256]{2,1,0:T(8,128)(2,1)S(1)}, u32[]{:S(2)}, u32[]{:S(2)}) async-start(bf16[8,96,256]{2,1,0:T(8,128)(2,1)} %shard_map.113), calls=%async_computation.4 | async-start | bytes 786432 | tf_op jit(solution)/shard_map/all_to_all | solution.py:312
  85.3 0.0 copy-done
  85.3 34.3 %shard_map.111 = bf16[8,96,256]{2,1,0:T(8,128)(2,1)} custom-call(s32[4,512]{1,0:T(4,128)} %bitcast.23, s32[2,512]{1,0:T(2,128)} %get-tuple-element.9.slots, s32[2,512]{1,0:T(2,128)} %get-tuple-element.10.oslots, bf16[768,16,128]{2,1,0:T(8,128)(2,1)} %fac.3, bf16[1536,256]{1,0:T(8,128)(2,1)} %bitcast.15, f32[2,8,256]{2,1,0:T(8,128)} %get-tuple-element.12.places, ...), custom_call_target="tpu_custom_call" | custom-call | tf_op jit(solution)/shard_map/pallas_call | solution.py:220
  119.7 0.0 all-to-all-done.4.second
  119.7 0.0 copy-start.2
  119.7 13.0 %all_to_all.32.first = bf16[8,96,256]{2,1,0:T(8,128)(2,1)} all-to-all(bf16[8,96,256]{2,1,0:T(8,128)(2,1)} %shard_map.111), channel_id=1, replica_groups=mesh['bra'=16,'ket'=8] {'ket'}, dimensions={0} | all-to-all | bytes 786432 | tf_op jit(solution)/shard_map/all_to_all | solution.py:312
  132.6 0.0 copy-done.2
  132.6 10.8 %shard_map.114 = f32[9216,128]{1,0:T(8,128)} custom-call(bf16[8,96,256]{2,1,0:T(8,128)(2,1)} %all_to_all.32.first, bf16[8,96,256]{2,1,0:T(8,128)(2,1)} %copy-done.2), custom_call_target="tpu_custom_call" | custom-call | tf_op jit(solution)/shard_map/pallas_call | solution.py:295
Async XLA Ops:
  24.2 16.1 %all-to-all-start.3 = ((bf16[16,96,256]{2,1,0:T(8,128)(2,1)}), bf16[16,96,256]{2,1,0:T(8,128)(2,1)S(1)}, u32[]{:S(2)}, u32[]{:S(2)}) async-start(bf16[16,96,256]{2,1,0:T(8,128)(2,1)} %bitcast.18), calls=%async_computation.3 | async-start | bytes 1572864 | tf_op jit(solution)/shard_map/all_to_all | solution.py:312
  40.3 3.6 %copy-start.1 = (bf16[16,96,256]{2,1,0:T(8,128)(2,1)}, bf16[16,96,256]{2,1,0:T(8,128)(2,1)S(1)}, u32[]{:S(2)}) copy-start(bf16[16,96,256]{2,1,0:T(8,128)(2,1)S(1)} %all-to-all-done.3) | copy-start | bytes 2359300
  40.3 37.9 %all-to-all-start.1 = ((bf16[16,96,256]{2,1,0:T(8,128)(2,1)}), bf16[16,96,256]{2,1,0:T(8,128)(2,1)S(1)}, u32[]{:S(2)}, u32[]{:S(2)}) async-start(bf16[16,96,256]{2,1,0:T(8,128)(2,1)} %bitcast.17), calls=%async_computation.1 | async-start | bytes 1572864 | tf_op jit(solution)/shard_map/all_to_all | solution.py:312
  78.2 7.1 %copy-start = (bf16[16,96,256]{2,1,0:T(8,128)(2,1)}, bf16[16,96,256]{2,1,0:T(8,128)(2,1)S(1)}, u32[]{:S(2)}) copy-start(bf16[16,96,256]{2,1,0:T(8,128)(2,1)S(1)} %all-to-all-done.1) | copy-start | bytes 2359300
  78.2 41.4 %all-to-all-start.4 = ((bf16[8,96,256]{2,1,0:T(8,128)(2,1)}), bf16[8,96,256]{2,1,0:T(8,128)(2,1)S(1)}, u32[]{:S(2)}, u32[]{:S(2)}) async-start(bf16[8,96,256]{2,1,0:T(8,128)(2,1)} %shard_map.113), calls=%async_computation.4 | async-start | bytes 786432 | tf_op jit(solution)/shard_map/all_to_all | solution.py:312
  119.7 13.0 %copy-start.2 = (bf16[8,96,256]{2,1,0:T(8,128)(2,1)}, bf16[8,96,256]{2,1,0:T(8,128)(2,1)S(1)}, u32[]{:S(2)}) copy-start(bf16[8,96,256]{2,1,0:T(8,128)(2,1)S(1)} %all-to-all-done.4.second) | copy-start | bytes 1179652

commit v2 on v1

--- a/solution.py
+++ b/solution.py
@@ -15,6 +15,8 @@
 HALF, CAPB, CAPK = 256, 96, 80
 OUTROWS = 96
 GROUP = 16
+PAIR = 4
+AHEAD = 8
 NB = ROWB * COLB
 VM = pl.BlockSpec(memory_space=pltpu.VMEM)
 SM = pl.BlockSpec(memory_space=pltpu.SMEM)
@@ -99,20 +101,16 @@
 def gather_kernel(half, ids, dens, out, wide, got):
     spread(dens, wide, NB)
 
-    def source(s, _):
+    for s in range(NBRA):
         count = ids[s, half * 128 + CAPB]
 
         def step(k, _):
-            for u in range(8):
-                p = k * 8 + u
-                r = ids[s, half * 128 + p]
-                got[pl.ds((s * CAPB + p) * 2, 2), :] = wide[pl.ds(r * 2, 2), :]
+            for u in range(16):
+                r = ids[s, half * 128 + u + k * 16]
+                got[pl.ds(pl.multiple_of(k * 32, 32) + (s * CAPB + u) * 2, 2), :] = wide[pl.ds(r * 2, 2), :]
             return 0
 
-        lax.fori_loop(0, (count + 7) // 8, step, 0)
-        return 0
-
-    lax.fori_loop(0, NBRA, source, 0)
+        lax.fori_loop(0, (count + 15) >> 4, step, 0)
 
     def pack(k, _):
         for u in range(4):
@@ -141,12 +139,13 @@
     spread_b = r[:, None] // 16 == lane[None, :] % 16
     sum_f = np.arange(16)[:, None] == r[None, :] // 16
     sum_b = r[:, None] // 16 == r[None, :] // 16
+    swap = r[None, :] == (r[:, None] % 16) * 16 + r[:, None] // 16
     keep_f = np.arange(16)[:, None] == lane[None, :] % 16
-    return [jnp.asarray(x, BF16) for x in (spread_b, sum_f, sum_b)] + [jnp.asarray(keep_f, F32)]
+    return [jnp.asarray(x, BF16) for x in (spread_b, sum_f, sum_b, swap)] + [jnp.asarray(keep_f, F32)]
 
 
 def eval_kernel(
-    half, tasks, slots, oslots, fac, fetched, places, spread_b, sum_f, sum_b, keep_f, out,
+    half, tasks, slots, oslots, fac, fetched, places, spread_b, sum_f, sum_b, swap, keep_f, out,
     rows, wide, outw, cd, jd, dsp, part, fin,
 ):
     base = half * HALF
@@ -177,21 +176,33 @@
             block = wide[pl.ds(slots[1, t] * 2, 2), :]
             jd[n * 16 : n * 16 + 16, 0:128] = (jnp.broadcast_to(block[0:1], (16, 128)) * keep).astype(BF16)
             jd[n * 16 : n * 16 + 16, 128:256] = (jnp.broadcast_to(block[1:2], (16, 128)) * keep).astype(BF16)
-        dsp[...] = jnp.dot(jd[...], spread_b[...], preferred_element_type=F32).astype(BF16)
+        dsp[...] = jnp.dot(jd[...], spread_b[...], preferred_element_type=F32)
         dcd = jnp.concatenate([cd[pl.ds(0, 16, stride=2), :], cd[pl.ds(1, 16, stride=2), :]], axis=1).astype(BF16)
+        dcd = jnp.dot(dcd, swap[...], preferred_element_type=F32).astype(BF16)
         acc = jnp.zeros((GROUP, BSZ), F32)
-        for n in range(GROUP):
+        def start(n):
             t = base + g * GROUP + n
             bra = pairs(tasks[0, t], tasks[1, t])
-            ket = pairs(tasks[2, t], tasks[3, t])
-            raw = nt_dot(ket, bra).astype(BF16)
-            tile = raw * lax.rsqrt(raw * raw + BF16(1.0))
-            coul = jnp.dot(dcd, tile, preferred_element_type=F32)
-            acc = jnp.where(iota((GROUP, BSZ), 0) == n, coul, acc)
-            dd = dsp[n * 16 : n * 16 + 16, :]
-            dd = jnp.concatenate([dd, dd], axis=1)
-            prod = jnp.concatenate([tile[16 * e : 16 * e + 16, :] * dd for e in range(16)], axis=0)
-            part[n * 16 : n * 16 + 16, :] = jnp.dot(sum_f[...], prod, preferred_element_type=F32).astype(BF16)
+            ket = pairs(tasks[3, t], tasks[2, t])
+            return nt_dot(ket, bra)
+
+        raws = {n: start(n) for n in range(AHEAD)}
+        for n0 in range(0, GROUP, PAIR):
+            for n in range(n0 + AHEAD, min(n0 + AHEAD + PAIR, GROUP)):
+                raws[n] = start(n)
+            for n in range(n0, n0 + PAIR):
+                raw = raws.pop(n).astype(BF16)
+                tile = raw * lax.rsqrt(raw * raw + BF16(1.0))
+                coul = jnp.dot(dcd, tile, preferred_element_type=F32)
+                acc = jnp.where(iota((GROUP, BSZ), 0) == n, coul, acc)
+                terms = []
+                for f in range(16):
+                    dd = jnp.broadcast_to(dsp[n * 16 + f : n * 16 + f + 1, :], (16, 128)).astype(BF16)
+                    dd = jnp.concatenate([dd, dd], axis=1)
+                    terms.append(tile[16 * f : 16 * f + 16, :] * dd)
+                while len(terms) > 1:
+                    terms = [x + y for x, y in zip(terms[0::2], terms[1::2])]
+                part[n * 16 : n * 16 + 16, :] = terms[0]
         full = jnp.dot(part[...], sum_b[...], preferred_element_type=F32)
         full = jnp.where((iota((256, 256), 0) % 16) == (iota((256, 256), 1) % 16), full, 0.0)
         exch = jnp.dot(sum_f[...], full.astype(BF16), preferred_element_type=F32) * (-0.5 * 0.0625)
@@ -220,7 +231,7 @@
     return pl.pallas_call(
         functools.partial(eval_kernel, half),
         out_shape=jax.ShapeDtypeStruct((NKET, OUTROWS, 256), BF16),
-        in_specs=[SM] * 3 + [VM] * 7,
+        in_specs=[SM] * 3 + [VM] * 8,
         out_specs=VM,
         scratch_shapes=[
             pltpu.VMEM((NBLK * FUNCS, RANK), F32),
@@ -228,7 +239,7 @@
             pltpu.VMEM((2 * NKET * CAPK, 128), F32),
             pltpu.VMEM((2 * GROUP, 128), F32),
             pltpu.VMEM((256, 256), BF16),
-            pltpu.VMEM((256, 128), BF16),
+            pltpu.VMEM((256, 128), F32),
             pltpu.VMEM((256, 256), BF16),
             pltpu.VMEM((4 * GROUP, 128), F32),
         ],
@@ -241,13 +252,13 @@
 
 def scatter_kernel(first, second, out, wide, where_v, where_s, sem, *accs):
     def clear(k, _):
-        for u in range(4):
-            r = pl.multiple_of((k * 4 + u) * 8, 8)
+        for u in range(16):
+            r = pl.multiple_of((k * 16 + u) * 8, 8)
             for acc in accs:
                 acc[pl.ds(r, 8), :] = jnp.zeros((8, 128), F32)
         return 0
 
-    lax.fori_loop(0, 2 * NB // 32, clear, 0)
+    lax.fori_loop(0, 2 * NB // 128, clear, 0)
     for h, src in enumerate((first, second)):
         for o in range(NKET):
             at = h * NKET + o
@@ -264,31 +275,27 @@
     copy.wait()
     per = 2 * NKET // SUMS
 
-    def source(s, _):
-        def step(k, _):
+    def add(k, _):
+        for s in range(per):
             for u in range(8):
-                p = k * 8 + u
                 for q, acc in enumerate(accs):
                     at = q * per + s
-                    r = where_s[at, p]
-                    acc[pl.ds(2 * r, 2), :] += wide[pl.ds((at * CAPK + p) * 2, 2), :]
-            return 0
-
-        lax.fori_loop(0, CAPK // 8, step, 0)
-        return 0
-
-    lax.fori_loop(0, per, source, 0)
+                    r = where_s[at, u + k * 8]
+                    acc[pl.ds(2 * r, 2), :] += wide[pl.ds(pl.multiple_of(k * 16, 16) + (at * CAPK + u) * 2, 2), :]
+        return 0
+
+    lax.fori_loop(0, CAPK // 8, add, 0)
 
     def total(k, _):
-        for u in range(4):
-            r = pl.multiple_of((k * 4 + u) * 8, 8)
+        for u in range(16):
+            r = pl.multiple_of((k * 16 + u) * 8, 8)
             v = accs[0][pl.ds(r, 8), :]
             for acc in accs[1:]:
                 v = v + acc[pl.ds(r, 8), :]
             out[pl.ds(r, 8), :] = v
         return 0
 
-    lax.fori_loop(0, 2 * NB // 32, total, 0)
+    lax.fori_loop(0, 2 * NB // 128, total, 0)
 
 
 def scatter(first, second):

time: 144 us -> 126 us (0.88)
  Pallas kernels: 93.1 us -> 74.5 us
    pallas_call x2, Pallas kernels: 68.6 us -> 52.4 us  [evaluate(): pl.pallas_call(functools.partial(eval_kernel, half), out_shape=jax.ShapeD...]
    pallas_call x1, Pallas kernels: 10.8 us -> 9.11 us  [scatter(): pl.pallas_call(scatter_kernel, out_shape=jax.ShapeDtypeStruct((2 * NB, 12...]
  transfers between devices with their start and end apart: 3 -> 3, of which waited for: 1 -> 1; matrix products, arithmetic and copies ran while one was open for 0% -> 0% of each run, Pallas kernels for 52% -> 46%
where the time goes in v2:
time: 126 us; the launch traced here: 125 us
  Pallas kernels  74.5 us (59%)
  blocking collectives  27.6 us (22%)
  starting transfers between devices  14.5 us (12%)
  waiting for transfers between devices  7.18 us (6%)
  local copies, waits for them, and re-layouts  1.34 us (1%)
    pallas_call x2, Pallas kernels, evaluate(): pl.pallas_call(functools.partial(eval_kernel, half), out_shape=jax.ShapeD...  52.4 us
    all_to_all x2, blocking collectives, exchange(): return lax.all_to_all(x, axis, split_axis=0, concat_axis=0, tiled=True)  27.6 us
    all_to_all x3, starting transfers between devices, exchange(): return lax.all_to_all(x, axis, split_axis=0, concat_axis=0, tiled=True)  14.5 us
    pallas_call x2, Pallas kernels, gather(): pl.pallas_call(functools.partial(gather_kernel, half), out_shape=jax.Shap...  10.7 us
    pallas_call x1, Pallas kernels, scatter(): pl.pallas_call(scatter_kernel, out_shape=jax.ShapeDtypeStruct((2 * NB, 12...  9.11 us
    all_to_all x3, waiting for transfers between devices, exchange(): return lax.all_to_all(x, axis, split_axis=0, concat_axis=0, tiled=True)  7.18 us
  transfers between devices with their start and end apart: 3, of which 1 were waited for; matrix products, arithmetic and copies ran while one was open for 0% of the time, Pallas kernels for 46%

profile of v2, /device:TPU:1, one launch (start us, length us, event | category | flops | bytes accessed | tf_op | source)
XLA Modules:
  0.0 125.1 jit_solution(13821636572643766499)
XLA Ops:
  0.0 2.3 %shard_map.127 = (s32[16,256]{1,0:T(8,128)}, s32[2,512]{1,0:T(2,128)}, s32[2,512]{1,0:T(2,128)}, f32[2,8,256]{2,1,0:T(8,128)}) custom-call(s32[4,512]{1,0:T(4,128)} %bitcast.21), custom_call_target="tpu_custom_call" | custom-call | tf_op jit(solution)/shard_map/pallas_call | solution.py:75
  2.3 0.7 copy.15
  3.1 14.8 %all_to_all.31 = s32[16,1,256]{2,1,0:T(1,128)S(1)} all-to-all(s32[16,1,256]{2,1,0:T(1,128)S(1)} %copy.15), channel_id=1, replica_groups=mesh['bra'=16,'ket'=8] {'bra'}, dimensions={0} | all-to-all | bytes 32768 | tf_op jit(solution)/shard_map/all_to_all | solution.py:319
  17.9 0.6 copy.19
  18.5 5.3 %shard_map.130 = bf16[1536,256]{1,0:T(8,128)(2,1)} custom-call(s32[16,256]{1,0:T(8,128)} %bitcast.19, bf16[4608,256]{1,0:T(8,128)(2,1)} %bitcast.13), custom_call_target="tpu_custom_call" | custom-call | tf_op jit(solution)/shard_map/pallas_call | solution.py:126
  23.8 3.6 %all-to-all-start.3 = ((bf16[16,96,256]{2,1,0:T(8,128)(2,1)}), bf16[16,96,256]{2,1,0:T(8,128)(2,1)S(1)}, u32[]{:S(2)}, u32[]{:S(2)}) async-start(bf16[16,96,256]{2,1,0:T(8,128)(2,1)} %bitcast.18), calls=%async_computation.3 | async-start | bytes 1572864 | tf_op jit(solution)/shard_map/all_to_all | solution.py:319
  27.4 5.4 %shard_map.128 = bf16[1536,256]{1,0:T(8,128)(2,1)} custom-call(s32[16,256]{1,0:T(8,128)} %bitcast.20, bf16[4608,256]{1,0:T(8,128)(2,1)} %bitcast.14), custom_call_target="tpu_custom_call" | custom-call | tf_op jit(solution)/shard_map/pallas_call | solution.py:126
  32.8 7.2 %all-to-all-done.3 = bf16[16,96,256]{2,1,0:T(8,128)(2,1)S(1)} async-done(((bf16[16,96,256]{2,1,0:T(8,128)(2,1)}), bf16[16,96,256]{2,1,0:T(8,128)(2,1)S(1)}, u32[]{:S(2)}, u32[]{:S(2)}) %all-to-all-start.3) | async-done | bytes 786464 | tf_op jit(solution)/shard_map/all_to_all | solution.py:319
  40.0 0.0 copy-start.1
  40.0 3.6 %all-to-all-start.1 = ((bf16[16,96,256]{2,1,0:T(8,128)(2,1)}), bf16[16,96,256]{2,1,0:T(8,128)(2,1)S(1)}, u32[]{:S(2)}, u32[]{:S(2)}) async-start(bf16[16,96,256]{2,1,0:T(8,128)(2,1)} %bitcast.17), calls=%async_computation.1 | async-start | bytes 1572864 | tf_op jit(solution)/shard_map/all_to_all | solution.py:319
  43.6 0.0 copy-done.1
  43.6 26.3 %shard_map.131 = bf16[8,96,256]{2,1,0:T(8,128)(2,1)} custom-call(s32[4,512]{1,0:T(4,128)} %bitcast.22, s32[2,512]{1,0:T(2,128)} %get-tuple-element.9.slots, s32[2,512]{1,0:T(2,128)} %get-tuple-element.10.oslots, bf16[768,16,128]{2,1,0:T(8,128)(2,1)} %fac.3, bf16[1536,256]{1,0:T(8,128)(2,1)} %bitcast.16, f32[2,8,256]{2,1,0:T(8,128)} %get-tuple-element.12.places, ...), custom_call_target="tpu_custom_call" | custom-call | tf_op jit(solution)/shard_map/pallas_call | solution.py:231
  69.9 0.0 all-to-all-done.1
  69.9 0.0 copy-start
  69.9 7.2 %all-to-all-start.4 = ((bf16[8,96,256]{2,1,0:T(8,128)(2,1)}), bf16[8,96,256]{2,1,0:T(8,128)(2,1)S(1)}, u32[]{:S(2)}, u32[]{:S(2)}) async-start(bf16[8,96,256]{2,1,0:T(8,128)(2,1)} %shard_map.131), calls=%async_computation.4 | async-start | bytes 786432 | tf_op jit(solution)/shard_map/all_to_all | solution.py:319
  77.2 0.0 copy-done
  77.2 26.0 %shard_map.129 = bf16[8,96,256]{2,1,0:T(8,128)(2,1)} custom-call(s32[4,512]{1,0:T(4,128)} %bitcast.23, s32[2,512]{1,0:T(2,128)} %get-tuple-element.9.slots, s32[2,512]{1,0:T(2,128)} %get-tuple-element.10.oslots, bf16[768,16,128]{2,1,0:T(8,128)(2,1)} %fac.3, bf16[1536,256]{1,0:T(8,128)(2,1)} %bitcast.15, f32[2,8,256]{2,1,0:T(8,128)} %get-tuple-element.12.places, ...), custom_call_target="tpu_custom_call" | custom-call | tf_op jit(solution)/shard_map/pallas_call | solution.py:231
  103.2 0.0 all-to-all-done.4.second
  103.2 0.0 copy-start.2
  103.2 12.8 %all_to_all.32.first = bf16[8,96,256]{2,1,0:T(8,128)(2,1)} all-to-all(bf16[8,96,256]{2,1,0:T(8,128)(2,1)} %shard_map.129), channel_id=1, replica_groups=mesh['bra'=16,'ket'=8] {'ket'}, dimensions={0} | all-to-all | bytes 786432 | tf_op jit(solution)/shard_map/all_to_all | solution.py:319
  116.0 0.0 copy-done.2
  116.0 9.1 %shard_map.132 = f32[9216,128]{1,0:T(8,128)} custom-call(bf16[8,96,256]{2,1,0:T(8,128)(2,1)} %all_to_all.32.first, bf16[8,96,256]{2,1,0:T(8,128)(2,1)} %copy-done.2), custom_call_target="tpu_custom_call" | custom-call | tf_op jit(solution)/shard_map/pallas_call | solution.py:302
Async XLA Ops:
  23.8 16.2 %all-to-all-start.3 = ((bf16[16,96,256]{2,1,0:T(8,128)(2,1)}), bf16[16,96,256]{2,1,0:T(8,128)(2,1)S(1)}, u32[]{:S(2)}, u32[]{:S(2)}) async-start(bf16[16,96,256]{2,1,0:T(8,128)(2,1)} %bitcast.18), calls=%async_computation.3 | async-start | bytes 1572864 | tf_op jit(solution)/shard_map/all_to_all | solution.py:319
  40.0 3.6 %copy-start.1 = (bf16[16,96,256]{2,1,0:T(8,128)(2,1)}, bf16[16,96,256]{2,1,0:T(8,128)(2,1)S(1)}, u32[]{:S(2)}) copy-start(bf16[16,96,256]{2,1,0:T(8,128)(2,1)S(1)} %all-to-all-done.3) | copy-start | bytes 2359300
  40.0 30.0 %all-to-all-start.1 = ((bf16[16,96,256]{2,1,0:T(8,128)(2,1)}), bf16[16,96,256]{2,1,0:T(8,128)(2,1)S(1)}, u32[]{:S(2)}, u32[]{:S(2)}) async-start(bf16[16,96,256]{2,1,0:T(8,128)(2,1)} %bitcast.17), calls=%async_computation.1 | async-start | bytes 1572864 | tf_op jit(solution)/shard_map/all_to_all | solution.py:319
  69.9 7.2 %copy-start = (bf16[16,96,256]{2,1,0:T(8,128)(2,1)}, bf16[16,96,256]{2,1,0:T(8,128)(2,1)S(1)}, u32[]{:S(2)}) copy-start(bf16[16,96,256]{2,1,0:T(8,128)(2,1)S(1)} %all-to-all-done.1) | copy-start | bytes 2359300
  69.9 33.3 %all-to-all-start.4 = ((bf16[8,96,256]{2,1,0:T(8,128)(2,1)}), bf16[8,96,256]{2,1,0:T(8,128)(2,1)S(1)}, u32[]{:S(2)}, u32[]{:S(2)}) async-start(bf16[8,96,256]{2,1,0:T(8,128)(2,1)} %shard_map.131), calls=%async_computation.4 | async-start | bytes 786432 | tf_op jit(solution)/shard_map/all_to_all | solution.py:319
  103.2 12.8 %copy-start.2 = (bf16[8,96,256]{2,1,0:T(8,128)(2,1)}, bf16[8,96,256]{2,1,0:T(8,128)(2,1)S(1)}, u32[]{:S(2)}) copy-start(bf16[8,96,256]{2,1,0:T(8,128)(2,1)S(1)} %all-to-all-done.4.second) | copy-start | bytes 1179652

commit v3 on v2

v3 whole, which is shorter than its diff:
```python
import functools

import jax
import jax.numpy as jnp
import numpy as np
from jax import lax
from jax.experimental import pallas as pl
from jax.experimental.pallas import tpu as pltpu
from jax.sharding import PartitionSpec as P

F32, BF16, I32 = jnp.float32, jnp.bfloat16, jnp.int32
FUNCS, RANK, BSZ = 16, 128, 256
NBLK, ROWB, COLB = 768, 48, 96
NBRA, NKET, TASKS = 16, 8, 512
CHUNK, CAPB, CAPK = 256, 192, 160
OUTROWS = 176
GROUP, LAG, LATE, AT = 16, 4, 4, 4
GROUPS = TASKS // GROUP
SAVED = 8
FRESH = GROUPS - SAVED
STORED = SAVED * GROUP
NB = ROWB * COLB
VM = pl.BlockSpec(memory_space=pltpu.VMEM)
SM = pl.BlockSpec(memory_space=pltpu.SMEM)
PARAMS = pltpu.CompilerParams(vmem_limit_bytes=56 * 1024 * 1024)


def iota(shape, dim):
    return lax.broadcasted_iota(I32, shape, dim)


def nt_dot(a, b):
    return lax.dot_general(a, b, (((1,), (1,)), ((), ())), preferred_element_type=F32)


def ranks(owners, count, upper, carry):
    marks = (iota((count, CHUNK), 0) == owners).astype(F32)
    before = jnp.dot(marks.astype(BF16), upper, preferred_element_type=F32) + carry
    place = jnp.sum(before * marks, axis=0, keepdims=True).astype(I32)
    return marks, place, carry + jnp.sum(marks, axis=1, keepdims=True)


def table(marks, place, value):
    at = (iota((256, CHUNK), 0) == place).astype(BF16)
    high = (value >> 6).astype(F32)
    low = (value & 63).astype(F32)
    return nt_dot((marks * high).astype(BF16), at), nt_dot((marks * low).astype(BF16), at)


def prep_kernel(tasks, ids, slots, oslots, places):
    upper = (iota((CHUNK, CHUNK), 0) < iota((CHUNK, CHUNK), 1)).astype(BF16)
    carry = jnp.zeros((NBRA, 1), F32)
    ocarry = jnp.zeros((NKET, 1), F32)
    high = low = ohigh = olow = 0.0
    for h in range(TASKS // CHUNK):
        cols = slice(h * CHUNK, (h + 1) * CHUNK)
        i, j, c, d = (tasks[r : r + 1, cols] for r in range(4))
        for k, s in enumerate((c, j)):
            own = lax.div(s, ROWB)
            marks, place, carry = ranks(own, NBRA, upper, carry)
            slots[k : k + 1, cols] = own * CAPB + place
            a, b = table(marks, place, lax.rem(s, ROWB) * COLB + (d >> 3))
            high, low = high + a, low + b
        for k, s in enumerate((j, c)):
            own = s & (NKET - 1)
            marks, place, ocarry = ranks(own, NKET, upper, ocarry)
            oslots[k : k + 1, cols] = own * CAPK + place
            a, b = table(marks, place, lax.rem(i, ROWB) * COLB + (s >> 3) + 1)
            ohigh, olow = ohigh + a, olow + b
    got = (high * 64.0 + low).astype(I32)
    ids[...] = jnp.where(iota((NBRA, 256), 1) < CAPB, got, carry.astype(I32))
    places[0] = ohigh
    places[1] = olow


def prep(tasks):
    return pl.pallas_call(
        prep_kernel,
        out_shape=(
            jax.ShapeDtypeStruct((NBRA, 256), I32),
            jax.ShapeDtypeStruct((2, TASKS), I32),
            jax.ShapeDtypeStruct((2, TASKS), I32),
            jax.ShapeDtypeStruct((2, NKET, 256), F32),
        ),
        in_specs=[VM],
        out_specs=(VM,) * 4,
        compiler_params=PARAMS,
    )(tasks)


def spread(src, dst, rows):
    def step(k, _):
        for u in range(4):
            r = pl.multiple_of(k * 64 + u * 16, 16)
            v = src[pl.ds(r, 16), :].astype(F32)
            dst[pl.ds(2 * r, 16, stride=2), :] = v[:, :128]
            dst[pl.ds(2 * r + 1, 16, stride=2), :] = v[:, 128:]
        return 0

    lax.fori_loop(0, rows // 64, step, 0)


def gather_kernel(ids, dens, out, wide, got):
    spread(dens, wide, NB)

    for s in range(NBRA):
        count = ids[s, CAPB]

        def step(k, _):
            for u in range(16):
                r = ids[s, u + k * 16]
                got[pl.ds(pl.multiple_of(k * 32, 32) + (s * CAPB + u) * 2, 2), :] = wide[pl.ds(r * 2, 2), :]
            return 0

        lax.fori_loop(0, (count + 15) >> 4, step, 0)

    def pack(k, _):
        for u in range(4):
            r = pl.multiple_of(k * 64 + u * 16, 16)
            out[pl.ds(r, 16), 0:128] = got[pl.ds(2 * r, 16, stride=2), :].astype(BF16)
            out[pl.ds(r, 16), 128:256] = got[pl.ds(2 * r + 1, 16, stride=2), :].astype(BF16)
        return 0

    lax.fori_loop(0, NBRA * CAPB // 64, pack, 0)


def gather(ids, dens):
    return pl.pallas_call(
        gather_kernel,
        out_shape=jax.ShapeDtypeStruct((NBRA * CAPB, 256), BF16),
        in_specs=[SM, VM],
        out_specs=VM,
        scratch_shapes=[pltpu.VMEM((2 * NB, 128), F32), pltpu.VMEM((2 * NBRA * CAPB, 128), F32)],
        compiler_params=PARAMS,
    )(ids, dens)


def constants():
    r = np.arange(256)
    lane = np.arange(128)
    spread_b = r[:, None] // 16 == lane[None, :] % 16
    sum_f = np.arange(16)[:, None] == r[None, :] // 16
    sum_b = r[:, None] // 16 == r[None, :] // 16
    swap = r[None, :] == (r[:, None] % 16) * 16 + r[:, None] // 16
    keep_f = np.arange(16)[:, None] == lane[None, :] % 16
    return [jnp.asarray(x, BF16) for x in (spread_b, sum_f, sum_b, swap)] + [jnp.asarray(keep_f, F32)]


def pairs(fac, rows, x, y):
    fy = fac[y]
    return jnp.concatenate(
        [
            jnp.broadcast_to(rows[pl.ds(x * FUNCS + a, 1), :], (FUNCS, RANK)).astype(BF16) * fy
            for a in range(FUNCS)
        ],
        axis=0,
    )


def start(tasks, fac, rows, t):
    bra = pairs(fac, rows, tasks[0, t], tasks[1, t])
    ket = pairs(fac, rows, tasks[3, t], tasks[2, t])
    return nt_dot(ket, bra)


def tile_of(raw):
    raw = raw.astype(BF16)
    return raw * lax.rsqrt(raw * raw + BF16(1.0))


def widen(fac, rows):
    def step(k, _):
        for u in range(16):
            rows[pl.ds(pl.multiple_of((k * 16 + u) * 16, 16), 16), :] = fac[k * 16 + u].astype(F32)
        return 0

    lax.fori_loop(0, NBLK // 16, step, 0)


UNROLL, LEAD = 16, 4


def tile_kernel(tasks, fac, after, tiles, rows, buf_a, buf_b, sem):
    widen(fac, rows)
    size = UNROLL * 256

    def copy(k, buf, which):
        return pltpu.make_async_copy(buf, tiles.at[pl.ds(pl.multiple_of(k * size, size), size)], sem.at[which])

    def step(m, _):
        for which, buf in enumerate((buf_a, buf_b)):
            k = 2 * m + which

            @pl.when(m > 0)
            def _():
                copy(k - 2, buf, which).wait()

            raws = {}
            for n in range(UNROLL + LEAD):
                if n < UNROLL:
                    raws[n] = start(tasks, fac, rows, TASKS - STORED + k * UNROLL + n)
                if n >= LEAD:
                    buf[(n - LEAD) * 256 : (n - LEAD) * 256 + 256, :] = tile_of(raws.pop(n - LEAD))
            copy(k, buf, which).start()
        return 0

    count = STORED // UNROLL
    lax.fori_loop(0, count // 2, step, 0)
    copy(count - 2, buf_a, 0).wait()
    copy(count - 1, buf_b, 1).wait()


def early_tiles(tasks, factors, after):
    return pl.pallas_call(
        tile_kernel,
        out_shape=pltpu.HBM((STORED * 256, 256), BF16),
        in_specs=[SM, VM, pl.BlockSpec(memory_space=pltpu.HBM)],
        out_specs=pl.BlockSpec(memory_space=pltpu.HBM),
        scratch_shapes=[
            pltpu.VMEM((NBLK * FUNCS, RANK), F32),
            pltpu.VMEM((UNROLL * 256, 256), BF16),
            pltpu.VMEM((UNROLL * 256, 256), BF16),
            pltpu.SemaphoreType.DMA((2,)),
        ],
        compiler_params=pltpu.CompilerParams(vmem_limit_bytes=24 * 1024 * 1024),
    )(tasks, factors, after)


def eval_kernel(
    tasks, slots, oslots, fac, saved, fetched, places, spread_b, sum_f, sum_b, swap, keep_f, out,
    rows, wide, outw, cd, jd, fin, stored, sem, *double,
):
    dsp, part, held, dcd, tiles = (double[k : k + 2] for k in range(0, 10, 2))

    def load(k):
        at = pl.ds(pl.multiple_of(k * (GROUP * 256), GROUP * 256), GROUP * 256)
        return pltpu.make_async_copy(saved.at[at], stored.at[at], sem.at[k])

    for k in range(SAVED):
        load(k).start()
    widen(fac, rows)
    spread(fetched, wide, NBRA * CAPB)
    keep = keep_f[...]

    def density(g, par):
        for n in range(GROUP):
            t = g * GROUP + n
            cd[2 * n : 2 * n + 2, :] = wide[pl.ds(slots[0, t] * 2, 2), :]
            block = wide[pl.ds(slots[1, t] * 2, 2), :]
            jd[n * 16 : n * 16 + 16, 0:128] = (jnp.broadcast_to(block[0:1], (16, 128)) * keep).astype(BF16)
            jd[n * 16 : n * 16 + 16, 128:256] = (jnp.broadcast_to(block[1:2], (16, 128)) * keep).astype(BF16)
        dsp[par][...] = jnp.dot(jd[...], spread_b[...], preferred_element_type=F32)
        both = jnp.concatenate([cd[pl.ds(0, 16, stride=2), :], cd[pl.ds(1, 16, stride=2), :]], axis=1).astype(BF16)
        dcd[par][...] = jnp.dot(both, swap[...], preferred_element_type=F32).astype(BF16)

    def deliver(g, par):
        full = jnp.dot(part[par][...], sum_b[...], preferred_element_type=F32)
        full = jnp.where((iota((256, 256), 0) & 15) == (iota((256, 256), 1) & 15), full, 0.0)
        exch = jnp.dot(sum_f[...], full.astype(BF16), preferred_element_type=F32) * (-0.5 * 0.0625)
        for k, v in enumerate((held[par][...] * 0.0625, exch)):
            fin[pl.ds(32 * k, 16, stride=2), :] = v[:, :128]
            fin[pl.ds(32 * k + 1, 16, stride=2), :] = v[:, 128:]
        for n in range(GROUP):
            t = g * GROUP + n
            for k in range(2):
                outw[pl.ds(oslots[k, t] * 2, 2), :] = fin[32 * k + 2 * n : 32 * k + 2 * n + 2, :]

    def stage(g, par, ahead=True, here=True, behind=True, blocks=True, ready=None):
        nxt = 1 - par
        raws = {}
        acc = jnp.zeros((GROUP, BSZ), F32)
        if here:
            coef = dcd[par][...]
        for s0 in range(0, GROUP + LAG, PAIR):
            for n in range(s0, s0 + PAIR):
                if ahead and n < GROUP:
                    raws[n] = start(tasks, fac, rows, (g + 1) * GROUP + n)
            if s0 == AT and behind:
                deliver(g - 1, nxt)
            if s0 == AT + PAIR and blocks:
                density(g + 1, nxt)
            for n in range(s0 - LAG, s0 - LAG + PAIR):
                if ahead and n >= 0:
                    tiles[nxt][n * 256 : n * 256 + 256, :] = tile_of(raws.pop(n))
            for n in range(s0 - LATE, s0 - LATE + PAIR):
                if here and 0 <= n < GROUP:
                    if ready is None:
                        tile = tiles[par][n * 256 : n * 256 + 256, :]
                    else:
                        tile = stored[pl.ds(pl.multiple_of(ready * (GROUP * 256), 256) + n * 256, 256), :]
                    coul = jnp.dot(coef, tile, preferred_element_type=F32)
                    acc = jnp.where(iota((GROUP, BSZ), 0) == n, coul, acc)
                    terms = []
                    for f in range(16):
                        dd = jnp.broadcast_to(dsp[par][n * 16 + f : n * 16 + f + 1, :], (16, 128)).astype(BF16)
                        dd = jnp.concatenate([dd, dd], axis=1)
                        terms.append(tile[16 * f : 16 * f + 16, :] * dd)
                    while len(terms) > 1:
                        terms = [x + y for x, y in zip(terms[0::2], terms[1::2])]
                    part[par][n * 16 : n * 16 + 16, :] = terms[0]
        if here:
            held[par][...] = acc

    stage(-1, 1, here=False, behind=False)
    stage(0, 0, behind=False)

    def step(m, _):
        stage(2 * m + 1, 1)
        stage(2 * m + 2, 0)
        return 0

    lax.fori_loop(0, (FRESH - 2) // 2, step, 0)
    stage(FRESH - 1, 1, ahead=False, blocks=SAVED > 0)
    if SAVED:

        def finish(m, _):
            for par in range(2):
                load(2 * m + par).wait()
                stage(FRESH + 2 * m + par, par, ahead=False, ready=2 * m + par)
            return 0

        lax.fori_loop(0, SAVED // 2 - 1, finish, 0)
        load(SAVED - 2).wait()
        stage(GROUPS - 2, 0, ahead=False, ready=SAVED - 2)
        load(SAVED - 1).wait()
        stage(GROUPS - 1, 1, ahead=False, blocks=False, ready=SAVED - 1)
    deliver(GROUPS - 1, 1)
    for o in range(NKET):
        for b in range(CAPK // 16):
            r = o * CAPK + b * 16
            for k in range(2):
                out[o, b * 16 : b * 16 + 16, 128 * k : 128 * k + 128] = outw[
                    pl.ds(2 * r + k, 16, stride=2), :
                ].astype(BF16)
        two = jnp.where(
            (iota((16, 256), 0) & 1) == 0,
            jnp.broadcast_to(places[0, o : o + 1, :], (16, 256)),
            jnp.broadcast_to(places[1, o : o + 1, :], (16, 256)),
        )
        out[o, CAPK:OUTROWS, :] = two.astype(BF16)


PAIR = 2


def evaluate(tasks, slots, oslots, factors, saved, fetched, places):
    return pl.pallas_call(
        eval_kernel,
        out_shape=jax.ShapeDtypeStruct((NKET, OUTROWS, 256), BF16),
        in_specs=[SM] * 3 + [VM, pl.BlockSpec(memory_space=pltpu.HBM)] + [VM] * 7,
        out_specs=VM,
        scratch_shapes=[
            pltpu.VMEM((NBLK * FUNCS, RANK), F32),
            pltpu.VMEM((2 * NBRA * CAPB, 128), F32),
            pltpu.VMEM((2 * NKET * CAPK, 128), F32),
            pltpu.VMEM((2 * GROUP, 128), F32),
            pltpu.VMEM((256, 256), BF16),
            pltpu.VMEM((4 * GROUP, 128), F32),
            pltpu.VMEM((max(STORED, 1) * 256, 256), BF16),
            pltpu.SemaphoreType.DMA((max(SAVED, 1),)),
        ]
        + [pltpu.VMEM((256, 128), F32)] * 2
        + [pltpu.VMEM((256, 256), BF16)] * 2
        + [pltpu.VMEM((GROUP, BSZ), F32)] * 2
        + [pltpu.VMEM((GROUP, BSZ), BF16)] * 2
        + [pltpu.VMEM((GROUP * 256, 256), BF16)] * 2,
        compiler_params=PARAMS,
    )(tasks, slots, oslots, factors, saved, fetched, places, *constants())


SUMS = 4


def scatter_kernel(blocks, out, wide, where_v, where_s, sem, out_sem, total, *accs):
    def clear(k, _):
        for u in range(16):
            r = pl.multiple_of((k * 16 + u) * 8, 8)
            for acc in accs:
                acc[pl.ds(r, 8), :] = jnp.zeros((8, 128), F32)
        return 0

    lax.fori_loop(0, 2 * NB // 128, clear, 0)
    for o in range(NKET):
        row = blocks[o, CAPK:OUTROWS, :].astype(F32)
        pos = (row[0:1] * 64.0 + row[1:2]).astype(I32) - 1
        where_v[o : o + 1, :] = jnp.where(pos < 0, NB, pos)
        for b in range(CAPK // 16):
            r = o * CAPK + b * 16
            v = blocks[o, b * 16 : b * 16 + 16, :].astype(F32)
            wide[pl.ds(2 * r, 16, stride=2), :] = v[:, :128]
            wide[pl.ds(2 * r + 1, 16, stride=2), :] = v[:, 128:]
    copy = pltpu.make_async_copy(where_v, where_s, sem)
    copy.start()
    copy.wait()
    per = NKET // SUMS

    def add(k, _):
        for s in range(per):
            for u in range(8):
                for q, acc in enumerate(accs):
                    at = q * per + s
                    r = where_s[at, u + k * 8]
                    acc[pl.ds(2 * r, 2), :] += wide[pl.ds(pl.multiple_of(k * 16, 16) + (at * CAPK + u) * 2, 2), :]
        return 0

    lax.fori_loop(0, CAPK // 8, add, 0)
    size = 2 * NB // PIECES
    copies = []
    for piece in range(PIECES):

        def gather_sums(k, _):
            for u in range(16):
                r = pl.multiple_of(piece * size + (k * 16 + u) * 8, 8)
                v = accs[0][pl.ds(r, 8), :]
                for acc in accs[1:]:
                    v = v + acc[pl.ds(r, 8), :]
                total[pl.ds(r, 8), :] = v
            return 0

        lax.fori_loop(0, size // 128, gather_sums, 0)
        part = pl.ds(piece * size, size)
        copies.append(pltpu.make_async_copy(total.at[part], out.at[part], out_sem.at[piece]))
        copies[-1].start()
    for copy in copies:
        copy.wait()


PIECES = 6


def scatter(blocks):
    return pl.pallas_call(
        scatter_kernel,
        out_shape=jax.ShapeDtypeStruct((2 * NB, 128), F32),
        in_specs=[VM],
        out_specs=pl.BlockSpec(memory_space=pl.ANY),
        scratch_shapes=[
            pltpu.VMEM((2 * NKET * CAPK, 128), F32),
            pltpu.VMEM((NKET, 256), I32),
            pltpu.SMEM((NKET, 256), I32),
            pltpu.SemaphoreType.DMA,
            pltpu.SemaphoreType.DMA((PIECES,)),
            pltpu.VMEM((2 * NB, 128), F32),
        ]
        + [pltpu.VMEM((2 * NB + 8, 128), F32)] * SUMS,
        compiler_params=PARAMS,
    )(blocks)


def exchange(x, axis):
    return lax.all_to_all(x, axis, split_axis=0, concat_axis=0, tiled=True)


def body(quartet_tasks, factors, density):
    tasks = quartet_tasks.reshape(TASKS, 4).T
    dens = density.reshape(NB, BSZ)
    ids, slots, oslots, places = prep(tasks)
    blocks = gather(exchange(ids, "bra"), dens).reshape(NBRA, CAPB, BSZ)
    fetched = exchange(blocks, "bra").reshape(NBRA * CAPB, BSZ)
    tiles = early_tiles(tasks, factors, pltpu.with_memory_space_constraint(blocks, pltpu.HBM))
    tiles = pltpu.with_memory_space_constraint(tiles, pltpu.HBM)
    parts = evaluate(tasks, slots, oslots, factors, tiles, fetched, places)
    fock = scatter(exchange(parts, "ket"))
    return fock.reshape(ROWB, COLB, 1, BSZ)


def solution(mesh):
    placed = (P("bra", "ket", None, None), P(), P("bra", None, "ket", None))
    return jax.shard_map(
        body, mesh=mesh, in_specs=placed, out_specs=P("bra", None, "ket", None), check_vma=False
    )
```

time: 126 us -> 121 us (0.960)
  starting transfers between devices: 14.5 us -> 4.42 us
  blocking collectives: 27.6 us -> 34.4 us
  Pallas kernels: 74.5 us -> 68.4 us
  waiting for transfers between devices: 7.18 us -> 10.4 us
    all_to_all x3 -> x1, starting transfers between devices: 14.5 us -> 4.42 us  [exchange(): return lax.all_to_all(x, axis, split_axis=0, concat_axis=0, tiled=True)]
    all_to_all x2, blocking collectives: 27.6 us -> 34.4 us  [exchange(): return lax.all_to_all(x, axis, split_axis=0, concat_axis=0, tiled=True)]
    pallas_call x4 -> x3, Pallas kernels: 63.1 us -> 57.6 us  [the longest x1 39.7 us: evaluate(): pl.pallas_call(eval_kernel, out_shape=jax.ShapeDtypeStruct((NKET, OUTROWS...]
    all_to_all x3 -> x1, waiting for transfers between devices: 7.18 us -> 10.4 us  [exchange(): return lax.all_to_all(x, axis, split_axis=0, concat_axis=0, tiled=True)]
  transfers between devices with their start and end apart: 3 -> 1, of which waited for: 1 -> 1; matrix products, arithmetic and copies ran while one was open for 0% -> 0% of each run, Pallas kernels for 46% -> 9%
where the time goes in v3:
time: 121 us; the launch traced here: 119 us
  Pallas kernels  68.4 us (57%)
  blocking collectives  34.4 us (28%)
  waiting for transfers between devices  10.4 us (9%)
  starting transfers between devices  4.42 us (4%)
  local copies, waits for them, and re-layouts  1.34 us (1%)
    pallas_call x1, Pallas kernels, evaluate(): pl.pallas_call(eval_kernel, out_shape=jax.ShapeDtypeStruct((NKET, OUTROWS...  39.7 us
    all_to_all x2, blocking collectives, exchange(): return lax.all_to_all(x, axis, split_axis=0, concat_axis=0, tiled=True)  34.4 us
    all_to_all x1, waiting for transfers between devices, exchange(): return lax.all_to_all(x, axis, split_axis=0, concat_axis=0, tiled=True)  10.4 us
    pallas_call x1, Pallas kernels, early_tiles(): pl.pallas_call(tile_kernel, out_shape=pltpu.HBM((STORED * 256, 256), BF16...  10.2 us
    pallas_call x1, Pallas kernels, scatter(): pl.pallas_call(scatter_kernel, out_shape=jax.ShapeDtypeStruct((2 * NB, 12...  7.94 us
    pallas_call x1, Pallas kernels, gather(): pl.pallas_call(gather_kernel, out_shape=jax.ShapeDtypeStruct((NBRA * CAPB...  7.59 us
    all_to_all x1, starting transfers between devices, exchange(): return lax.all_to_all(x, axis, split_axis=0, concat_axis=0, tiled=True)  4.42 us
    pallas_call x1, Pallas kernels, prep(): pl.pallas_call(prep_kernel, out_shape=(jax.ShapeDtypeStruct((NBRA, 256),...  2.92 us
  transfers between devices with their start and end apart: 1, of which 1 were waited for; matrix products, arithmetic and copies ran while one was open for 0% of the time, Pallas kernels for 9%

profile of v3, /device:TPU:1, one launch (start us, length us, event | category | flops | bytes accessed | tf_op | source)
XLA Modules:
  0.0 119.0 jit_solution(1097191738467769828)
XLA Ops:
  0.0 2.9 %shard_map.82 = (s32[16,256]{1,0:T(8,128)}, s32[2,512]{1,0:T(2,128)}, s32[2,512]{1,0:T(2,128)}, f32[2,8,256]{2,1,0:T(8,128)}) custom-call(s32[4,512]{1,0:T(4,128)} %bitcast.11), custom_call_target="tpu_custom_call" | custom-call | tf_op jit(solution)/shard_map/pallas_call | solution.py:77
  2.9 0.7 copy.10
  3.7 14.8 %all_to_all.21 = s32[16,1,256]{2,1,0:T(1,128)S(1)} all-to-all(s32[16,1,256]{2,1,0:T(1,128)S(1)} %copy.10), channel_id=1, replica_groups=mesh['bra'=16,'ket'=8] {'bra'}, dimensions={0} | all-to-all | bytes 32768 | tf_op jit(solution)/shard_map/all_to_all | solution.py:451
  18.5 0.6 copy.14
  19.1 0.0 copy-start
  19.1 0.0 copy-start.1
  19.1 7.6 %shard_map.83 = bf16[3072,256]{1,0:T(8,128)(2,1)} custom-call(s32[16,256]{1,0:T(8,128)} %bitcast.17, bf16[4608,256]{1,0:T(8,128)(2,1)} %bitcast.16), custom_call_target="tpu_custom_call" | custom-call | tf_op jit(solution)/shard_map/pallas_call | solution.py:128
  26.7 4.4 %all-to-all-start.1 = ((bf16[16,192,256]{2,1,0:T(8,128)(2,1)}), bf16[16,192,256]{2,1,0:T(8,128)(2,1)}, u32[]{:S(2)}, u32[]{:S(2)}) async-start(bf16[16,192,256]{2,1,0:T(8,128)(2,1)} %bitcast.14), calls=%async_computation.1 | async-start | bytes 3145728 | tf_op jit(solution)/shard_map/all_to_all | solution.py:451
  31.1 0.0 copy-done
  31.1 0.0 copy-done.1
  31.1 10.2 %shard_map.84.saved = bf16[32768,256]{1,0:T(8,128)(2,1)} custom-call(s32[4,512]{1,0:T(4,128)S(1)} %bitcast.13, bf16[768,16,128]{2,1,0:T(8,128)(2,1)S(1)} %copy-done, bf16[16,192,256]{2,1,0:T(8,128)(2,1)} %bitcast.15), custom_call_target="tpu_custom_call" | custom-call | tf_op jit(solution)/shard_map/pallas_call | solution.py:214
  41.4 10.4 %all-to-all-done.1 = bf16[16,192,256]{2,1,0:T(8,128)(2,1)} async-done(((bf16[16,192,256]{2,1,0:T(8,128)(2,1)}), bf16[16,192,256]{2,1,0:T(8,128)(2,1)}, u32[]{:S(2)}, u32[]{:S(2)}) %all-to-all-start.1) | async-done | bytes 1572896 | tf_op jit(solution)/shard_map/all_to_all | solution.py:451
  51.7 39.7 %shard_map.85 = bf16[8,176,256]{2,1,0:T(8,128)(2,1)} custom-call(s32[4,512]{1,0:T(4,128)} %bitcast.12, s32[2,512]{1,0:T(2,128)} %get-tuple-element.9.slots, s32[2,512]{1,0:T(2,128)} %get-tuple-element.10.oslots, bf16[768,16,128]{2,1,0:T(8,128)(2,1)} %fac.3, bf16[32768,256]{1,0:T(8,128)(2,1)} %shard_map.84.saved, bf16[3072,256]{1,0:T(8,128)(2,1)} %bitcast.6.fetched, ...), custom_call_target="tpu_custom_call" | custom-call | tf_op jit(solution)/shard_map/pallas_call | solution.py:347
  91.5 19.6 %all_to_all.22.blocks = bf16[8,176,256]{2,1,0:T(8,128)(2,1)} all-to-all(bf16[8,176,256]{2,1,0:T(8,128)(2,1)} %shard_map.85), channel_id=1, replica_groups=mesh['bra'=16,'ket'=8] {'ket'}, dimensions={0} | all-to-all | bytes 1441792 | tf_op jit(solution)/shard_map/all_to_all | solution.py:451
  111.0 7.9 %shard_map.86 = f32[9216,128]{1,0:T(8,128)} custom-call(bf16[8,176,256]{2,1,0:T(8,128)(2,1)} %all_to_all.22.blocks), custom_call_target="tpu_custom_call" | custom-call | tf_op jit(solution)/shard_map/pallas_call | solution.py:432
Async XLA Ops:
  19.1 12.0 %copy-start = (bf16[768,16,128]{2,1,0:T(8,128)(2,1)S(1)}, bf16[768,16,128]{2,1,0:T(8,128)(2,1)}, u32[]{:S(2)}) copy-start(bf16[768,16,128]{2,1,0:T(8,128)(2,1)} %fac.3) | copy-start | bytes 9437188
  19.1 12.0 %copy-start.1 = (s32[1,1,512,4]{2,3,1,0:T(4,128)S(1)}, s32[1,1,512,4]{2,3,1,0:T(4,128)}, u32[]{:S(2)}) copy-start(s32[1,1,512,4]{2,3,1,0:T(4,128)} %param.8) | copy-start | bytes 24580
  26.7 25.0 %all-to-all-start.1 = ((bf16[16,192,256]{2,1,0:T(8,128)(2,1)}), bf16[16,192,256]{2,1,0:T(8,128)(2,1)}, u32[]{:S(2)}, u32[]{:S(2)}) async-start(bf16[16,192,256]{2,1,0:T(8,128)(2,1)} %bitcast.14), calls=%async_computation.1 | async-start | bytes 3145728 | tf_op jit(solution)/shard_map/all_to_all | solution.py:451

commit v4 on v3

--- a/solution.py
+++ b/solution.py
@@ -16,13 +16,13 @@
 OUTROWS = 176
 GROUP, LAG, LATE, AT = 16, 4, 4, 4
 GROUPS = TASKS // GROUP
-SAVED = 8
+SAVED = 14
 FRESH = GROUPS - SAVED
 STORED = SAVED * GROUP
 NB = ROWB * COLB
 VM = pl.BlockSpec(memory_space=pltpu.VMEM)
 SM = pl.BlockSpec(memory_space=pltpu.SMEM)
-PARAMS = pltpu.CompilerParams(vmem_limit_bytes=56 * 1024 * 1024)
+PARAMS = pltpu.CompilerParams(vmem_limit_bytes=58 * 1024 * 1024)
 
 
 def iota(shape, dim):
@@ -47,45 +47,60 @@
     return nt_dot((marks * high).astype(BF16), at), nt_dot((marks * low).astype(BF16), at)
 
 
-def prep_kernel(tasks, ids, slots, oslots, places):
+def ask_kernel(tasks, ids, slots):
     upper = (iota((CHUNK, CHUNK), 0) < iota((CHUNK, CHUNK), 1)).astype(BF16)
     carry = jnp.zeros((NBRA, 1), F32)
-    ocarry = jnp.zeros((NKET, 1), F32)
-    high = low = ohigh = olow = 0.0
+    high = low = 0.0
     for h in range(TASKS // CHUNK):
         cols = slice(h * CHUNK, (h + 1) * CHUNK)
-        i, j, c, d = (tasks[r : r + 1, cols] for r in range(4))
-        for k, s in enumerate((c, j)):
+        for k, s in enumerate((tasks[2:3, cols], tasks[1:2, cols])):
             own = lax.div(s, ROWB)
             marks, place, carry = ranks(own, NBRA, upper, carry)
             slots[k : k + 1, cols] = own * CAPB + place
-            a, b = table(marks, place, lax.rem(s, ROWB) * COLB + (d >> 3))
+            a, b = table(marks, place, lax.rem(s, ROWB) * COLB + (tasks[3:4, cols] >> 3))
             high, low = high + a, low + b
-        for k, s in enumerate((j, c)):
-            own = s & (NKET - 1)
-            marks, place, ocarry = ranks(own, NKET, upper, ocarry)
-            oslots[k : k + 1, cols] = own * CAPK + place
-            a, b = table(marks, place, lax.rem(i, ROWB) * COLB + (s >> 3) + 1)
-            ohigh, olow = ohigh + a, olow + b
     got = (high * 64.0 + low).astype(I32)
     ids[...] = jnp.where(iota((NBRA, 256), 1) < CAPB, got, carry.astype(I32))
-    places[0] = ohigh
-    places[1] = olow
-
-
-def prep(tasks):
-    return pl.pallas_call(
-        prep_kernel,
-        out_shape=(
-            jax.ShapeDtypeStruct((NBRA, 256), I32),
-            jax.ShapeDtypeStruct((2, TASKS), I32),
-            jax.ShapeDtypeStruct((2, TASKS), I32),
-            jax.ShapeDtypeStruct((2, NKET, 256), F32),
-        ),
+
+
+def send_kernel(tasks, after, oslots, places):
+    upper = (iota((CHUNK, CHUNK), 0) < iota((CHUNK, CHUNK), 1)).astype(BF16)
+    carry = jnp.zeros((NKET, 1), F32)
+    high = low = 0.0
+    for h in range(TASKS // CHUNK):
+        cols = slice(h * CHUNK, (h + 1) * CHUNK)
+        for k, s in enumerate((tasks[1:2, cols], tasks[2:3, cols])):
+            own = s & (NKET - 1)
+            marks, place, carry = ranks(own, NKET, upper, carry)
+            oslots[k : k + 1, cols] = own * CAPK + place
+            a, b = table(marks, place, lax.rem(tasks[0:1, cols], ROWB) * COLB + (s >> 3) + 1)
+            high, low = high + a, low + b
+    places[0] = high
+    places[1] = low
+
+
+SMALL = pltpu.CompilerParams(vmem_limit_bytes=16 * 1024 * 1024)
+PAIRS = jax.ShapeDtypeStruct((2, TASKS), I32)
+
+
+def ask(tasks):
+    return pl.pallas_call(
+        ask_kernel,
+        out_shape=(jax.ShapeDtypeStruct((NBRA, 256), I32), PAIRS),
         in_specs=[VM],
-        out_specs=(VM,) * 4,
-        compiler_params=PARAMS,
+        out_specs=(VM, VM),
+        compiler_params=SMALL,
     )(tasks)
+
+
+def send(tasks, after):
+    return pl.pallas_call(
+        send_kernel,
+        out_shape=(PAIRS, jax.ShapeDtypeStruct((2, NKET, 256), F32)),
+        in_specs=[VM, pl.BlockSpec(memory_space=pltpu.HBM)],
+        out_specs=(VM, VM),
+        compiler_params=SMALL,
+    )(tasks, after)
 
 
 def spread(src, dst, rows):
@@ -131,7 +146,7 @@
         in_specs=[SM, VM],
         out_specs=VM,
         scratch_shapes=[pltpu.VMEM((2 * NB, 128), F32), pltpu.VMEM((2 * NBRA * CAPB, 128), F32)],
-        compiler_params=PARAMS,
+        compiler_params=SMALL,
     )(ids, dens)
 
 
@@ -443,7 +458,7 @@
             pltpu.VMEM((2 * NB, 128), F32),
         ]
         + [pltpu.VMEM((2 * NB + 8, 128), F32)] * SUMS,
-        compiler_params=PARAMS,
+        compiler_params=pltpu.CompilerParams(vmem_limit_bytes=32 * 1024 * 1024),
     )(blocks)
 
 
@@ -454,12 +469,13 @@
 def body(quartet_tasks, factors, density):
     tasks = quartet_tasks.reshape(TASKS, 4).T
     dens = density.reshape(NB, BSZ)
-    ids, slots, oslots, places = prep(tasks)
+    ids, slots = ask(tasks)
     blocks = gather(exchange(ids, "bra"), dens).reshape(NBRA, CAPB, BSZ)
     fetched = exchange(blocks, "bra").reshape(NBRA * CAPB, BSZ)
-    tiles = early_tiles(tasks, factors, pltpu.with_memory_space_constraint(blocks, pltpu.HBM))
-    tiles = pltpu.with_memory_space_constraint(tiles, pltpu.HBM)
-    parts = evaluate(tasks, slots, oslots, factors, tiles, fetched, places)
+    gathered = pltpu.with_memory_space_constraint(blocks, pltpu.HBM)
+    oslots, places = send(tasks, gathered)
+    saved = pltpu.with_memory_space_constraint(early_tiles(tasks, factors, gathered), pltpu.HBM)
+    parts = evaluate(tasks, slots, oslots, factors, saved, fetched, places)
     fock = scatter(exchange(parts, "ket"))
     return fock.reshape(ROWB, COLB, 1, BSZ)
 

time: 121 us -> 114 us (0.942); the launches traced: 119 us -> 114 us
  waiting for transfers between devices: 10.4 us -> 2.03 us
  local copies, waits for them, and re-layouts: 1.34 us -> 3.61 us
    all_to_all x1, waiting for transfers between devices: 10.4 us -> 2.03 us  [exchange(): return lax.all_to_all(x, axis, split_axis=0, concat_axis=0, tiled=True)]
    pallas_call x1, Pallas kernels: 10.2 us -> 16.5 us  [early_tiles(): pl.pallas_call(tile_kernel, out_shape=pltpu.HBM((STORED * 256, 256), BF16...]
    pallas_call x1, Pallas kernels: 39.7 us -> 36.5 us  [evaluate(): pl.pallas_call(eval_kernel, out_shape=jax.ShapeDtypeStruct((NKET, OUTROWS...]
    unnamed x5 -> x15, local copies, waits for them, and re-layouts: 0.61 us -> 3.59 us
    pallas_call x1 -> x2, Pallas kernels: 2.92 us -> 1.69 us  [the longest x1 0.85 us: ask(): pl.pallas_call(ask_kernel, out_shape=(jax.ShapeDtypeStruct((NBRA, 256), I...]
  transfers between devices with their start and end apart: 1 -> 1, of which waited for: 1 -> 1; matrix products, arithmetic and copies ran while one was open for 0% -> 0% of each run, Pallas kernels for 9% -> 15%
where the time goes in v4:
time: 114 us
  Pallas kernels  67.9 us (60%)
  blocking collectives  35.3 us (31%)
  starting transfers between devices  4.68 us (4%)
  local copies, waits for them, and re-layouts  3.61 us (3%)
  waiting for transfers between devices  2.03 us (2%)
    pallas_call x1, Pallas kernels, evaluate(): pl.pallas_call(eval_kernel, out_shape=jax.ShapeDtypeStruct((NKET, OUTROWS...  36.5 us
    all_to_all x2, blocking collectives, exchange(): return lax.all_to_all(x, axis, split_axis=0, concat_axis=0, tiled=True)  35.3 us
    pallas_call x1, Pallas kernels, early_tiles(): pl.pallas_call(tile_kernel, out_shape=pltpu.HBM((STORED * 256, 256), BF16...  16.5 us
    pallas_call x1, Pallas kernels, scatter(): pl.pallas_call(scatter_kernel, out_shape=jax.ShapeDtypeStruct((2 * NB, 12...  6.83 us
    pallas_call x1, Pallas kernels, gather(): pl.pallas_call(gather_kernel, out_shape=jax.ShapeDtypeStruct((NBRA * CAPB...  6.42 us
    all_to_all x1, starting transfers between devices, exchange(): return lax.all_to_all(x, axis, split_axis=0, concat_axis=0, tiled=True)  4.68 us
    unnamed x15, local copies, waits for them, and re-layouts  3.59 us
  transfers between devices with their start and end apart: 1, of which 1 were waited for; matrix products, arithmetic and copies ran while one was open for 0% of the time, Pallas kernels for 15%

profile of v4, /device:TPU:1, one launch (start us, length us, event | category | flops | bytes accessed | tf_op | source)
XLA Modules:
  0.0 113.6 jit_solution(11615072935571150519)
XLA Ops:
  0.0 0.0 copy-start.2
  0.0 0.7 copy-done.2
  0.7 0.9 shard_map.82
  1.6 0.0 copy-start.5
  1.6 14.8 %all_to_all.21 = s32[16,1,256]{2,1,0:T(1,128)S(1)} all-to-all(s32[16,1,256]{2,1,0:T(1,128)S(1)} %copy.10), channel_id=1, replica_groups=mesh['bra'=16,'ket'=8] {'bra'}, dimensions={0} | all-to-all | bytes 32768 | tf_op jit(solution)/shard_map/all_to_all | solution.py:466
  16.4 0.0 copy-done.5
  16.4 0.0 copy-start.1
  16.4 1.7 %copy-done.1 = bf16[48,96,1,256]{3,1,2,0:T(8,128)(2,1)S(1)} copy-done((bf16[48,96,1,256]{3,1,2,0:T(8,128)(2,1)S(1)}, bf16[48,96,1,256]{3,1,2,0:T(8,128)(2,1)}, u32[]{:S(2)}) %copy-start.1) | copy-done | bytes 2359320
  18.1 0.0 copy-start.3
  18.1 6.4 %shard_map.83 = bf16[3072,256]{1,0:T(8,128)(2,1)} custom-call(s32[16,256]{1,0:T(8,128)S(1)} %bitcast.16, bf16[4608,256]{1,0:T(8,128)(2,1)S(1)} %bitcast.11), custom_call_target="tpu_custom_call" | custom-call | tf_op jit(solution)/shard_map/pallas_call | solution.py:143
  24.5 0.0 copy-start
  24.5 4.7 %all-to-all-start.1 = ((bf16[16,192,256]{2,1,0:T(8,128)(2,1)}), bf16[16,192,256]{2,1,0:T(8,128)(2,1)}, u32[]{:S(2)}, u32[]{:S(2)}) async-start(bf16[16,192,256]{2,1,0:T(8,128)(2,1)} %bitcast.5.after), calls=%async_computation.1 | async-start | bytes 3145728 | tf_op jit(solution)/shard_map/all_to_all | solution.py:466
  29.2 0.0 copy-done.3
  29.2 0.8 shard_map.84
  30.1 0.0 copy-start.4
  30.1 0.6 copy-done.4
  30.7 0.0 copy-start.6
  30.7 0.6 copy-done.6
  31.3 0.0 copy-done
  31.3 16.5 %shard_map.85.saved = bf16[57344,256]{1,0:T(8,128)(2,1)} custom-call(s32[4,512]{1,0:T(4,128)S(1)} %bitcast.15, bf16[768,16,128]{2,1,0:T(8,128)(2,1)S(1)} %copy-done, bf16[16,192,256]{2,1,0:T(8,128)(2,1)} %bitcast.5.after), custom_call_target="tpu_custom_call" | custom-call | tf_op jit(solution)/shard_map/pallas_call | solution.py:229
  47.8 2.0 %all-to-all-done.1 = bf16[16,192,256]{2,1,0:T(8,128)(2,1)} async-done(((bf16[16,192,256]{2,1,0:T(8,128)(2,1)}), bf16[16,192,256]{2,1,0:T(8,128)(2,1)}, u32[]{:S(2)}, u32[]{:S(2)}) %all-to-all-start.1) | async-done | bytes 1572896 | tf_op jit(solution)/shard_map/all_to_all | solution.py:466
  49.8 36.5 %shard_map.86 = bf16[8,176,256]{2,1,0:T(8,128)(2,1)} custom-call(s32[4,512]{1,0:T(4,128)} %bitcast.12, s32[2,512]{1,0:T(2,128)} %copy-done.5, s32[2,512]{1,0:T(2,128)} %copy-done.6, bf16[768,16,128]{2,1,0:T(8,128)(2,1)} %fac.3, bf16[57344,256]{1,0:T(8,128)(2,1)} %shard_map.85.saved, bf16[3072,256]{1,0:T(8,128)(2,1)} %bitcast.6.fetched, ...), custom_call_target="tpu_custom_call" | custom-call | tf_op jit(solution)/shard_map/pallas_call | solution.py:362
  86.3 20.5 %all_to_all.22.blocks = bf16[8,176,256]{2,1,0:T(8,128)(2,1)S(1)} all-to-all(bf16[8,176,256]{2,1,0:T(8,128)(2,1)} %shard_map.86), channel_id=1, replica_groups=mesh['bra'=16,'ket'=8] {'ket'}, dimensions={0} | all-to-all | bytes 1441792 | tf_op jit(solution)/shard_map/all_to_all | solution.py:466
  106.8 6.8 %shard_map.87 = f32[9216,128]{1,0:T(8,128)} custom-call(bf16[8,176,256]{2,1,0:T(8,128)(2,1)S(1)} %all_to_all.22.blocks), custom_call_target="tpu_custom_call" | custom-call | tf_op jit(solution)/shard_map/pallas_call | solution.py:447
  (2 shorter events, 0.0 us)
Async XLA Ops:
  0.0 0.7 copy-start.2
  1.6 14.9 %copy-start.5 = (s32[2,512]{1,0:T(2,128)}, s32[2,512]{1,0:T(2,128)S(1)}, u32[]{:S(2)}) copy-start(s32[2,512]{1,0:T(2,128)S(1)} %get-tuple-element.9.slots) | copy-start | bytes 12292
  16.4 1.7 %copy-start.1 = (bf16[48,96,1,256]{3,1,2,0:T(8,128)(2,1)S(1)}, bf16[48,96,1,256]{3,1,2,0:T(8,128)(2,1)}, u32[]{:S(2)}) copy-start(bf16[48,96,1,256]{3,1,2,0:T(8,128)(2,1)} %param.10) | copy-start | bytes 7077892
  18.1 11.1 %copy-start.3 = (s32[1,1,512,4]{2,3,1,0:T(4,128)S(1)}, s32[1,1,512,4]{2,3,1,0:T(4,128)}, u32[]{:S(2)}) copy-start(s32[1,1,512,4]{2,3,1,0:T(4,128)} %param.8) | copy-start | bytes 24580
  24.5 6.8 %copy-start = (bf16[768,16,128]{2,1,0:T(8,128)(2,1)S(1)}, bf16[768,16,128]{2,1,0:T(8,128)(2,1)}, u32[]{:S(2)}) copy-start(bf16[768,16,128]{2,1,0:T(8,128)(2,1)} %fac.3) | copy-start | bytes 9437188
  24.5 25.3 %all-to-all-start.1 = ((bf16[16,192,256]{2,1,0:T(8,128)(2,1)}), bf16[16,192,256]{2,1,0:T(8,128)(2,1)}, u32[]{:S(2)}, u32[]{:S(2)}) async-start(bf16[16,192,256]{2,1,0:T(8,128)(2,1)} %bitcast.5.after), calls=%async_computation.1 | async-start | bytes 3145728 | tf_op jit(solution)/shard_map/all_to_all | solution.py:466
  30.1 0.6 copy-start.4
  30.7 0.6 copy-start.6
